TPU v7x, 128 devices: a whole 4x4x4 slice. The times are simulated.
128 devices in a mesh: dp: 16 (over x, y_hi, core), hp: 8 (over z, y_lo).
Axes of the slice: x: 4, y: 4 (y_hi: 2, y_lo: 2; y = y_hi * 2 + y_lo), z: 4, core: 2. Of those that a mesh axis runs over, the one named last changes fastest.
Arguments:
- residual: bfloat16 [512, 7168], P('dp', 'hp'), may hold values from -60 to 60
- queries: bfloat16 [512, 128, 192], P('dp', 'hp'), may hold values from -48 to 48
- latent_cache: bfloat16 [512, 512, 576], P('dp'), may hold values from -4 to 4
- new_latent: bfloat16 [512, 576], P('dp'), may hold values from -4 to 4
- lengths: int32 [512], P('dp'), may hold values from 1 to 512, as said below
- w_absorb: bfloat16 [128, 128, 512], P('hp'), may hold values from -0.5 to 0.5
- w_value: bfloat16 [128, 512, 128], P('hp'), may hold values from -0.25 to 0.25
- w_out: bfloat16 [16384, 8, 896], P('hp', None, 'dp'), may hold values from -0.046875 to 0.046875
- norm_gain: bfloat16 [7168], P('hp'), may hold values from 0.099609375 to 1.8984375
- w_gate: bfloat16 [7168, 18432], P('hp', 'dp'), may hold values from -0.0625 to 0.0625
- w_up: bfloat16 [7168, 18432], P('hp', 'dp'), may hold values from -0.0625 to 0.0625
- w_down: bfloat16 [18432, 7168], P('dp', 'hp'), may hold values from -0.046875 to 0.046875
Outputs:
- layer_out: bfloat16 [512, 7168], P('dp', 'hp')
Inputs may be any that keep to these rules, and one draw needn't show every extreme that they name: `lengths`: some sample holds all 512 slots in every draw.
All inputs are finite; a program needn't handle non-finite values.
Results may differ from a plain program's by a relative error of at most 0.014.
Values may be sent and summed in bfloat16 or wider, within the bound.
No kernel may reach another device: no remote copies, remote signals or barrier semaphores. Data moves between devices by JAX's collectives and lax.ppermute only.
A program may use at most 128 MiB of HBM per device.

v0:
```python
import math

import jax
import jax.numpy as jnp
from jax import lax
from jax.sharding import PartitionSpec as P

D = 7168


def from_everyone(x, axis):
    devices = lax.axis_size(axis)
    return lax.all_to_all(jnp.broadcast_to(x[None], (devices, *x.shape)), axis, 0, 0, tiled=True)


def laid_out(pieces, dim):
    pieces = jnp.moveaxis(pieces, 0, dim)
    lengths = pieces.shape
    return pieces.reshape(*lengths[:dim], lengths[dim] * lengths[dim + 1], *lengths[dim + 2 :])


def collect(x, axis, dim):
    pieces = from_everyone(x, axis)
    return laid_out(pieces, dim)


def in_blocks(x, dim, devices):
    lengths = x.shape
    pieces = x.reshape(*lengths[:dim], devices, lengths[dim] // devices, *lengths[dim + 1 :])
    return jnp.moveaxis(pieces, dim, 0)


def sum_at_owner(x, axis, dim):
    pieces = in_blocks(x, dim, lax.axis_size(axis))
    arrived = lax.all_to_all(pieces, axis, split_axis=0, concat_axis=0, tiled=True)
    return arrived.astype(jnp.float32).sum(axis=0)


def over_copies(x, axis):
    everything = from_everyone(x, axis)
    return jnp.sum(everything, axis=0)


def side_by_side(arrays, axis, dim, along):
    ends, at = ([], 0)
    for a in arrays[:-1]:
        at += a.shape[along]
        ends.append(at)
    both = jnp.concatenate(arrays, axis=along)
    return tuple(
        jnp.split(lax.psum_scatter(both, axis, scatter_dimension=dim, tiled=True), ends, axis=along)
    )


def on_device(
    residual,
    queries,
    latent_cache,
    new_latent,
    lengths,
    w_absorb,
    w_value,
    w_out,
    norm_gain,
    w_gate,
    w_up,
    w_down,
):
    sample_rows = queries.shape[0]
    nope_width = w_absorb.shape[1]
    latent_width = w_absorb.shape[2]
    softmax_scale = 1.0 / math.sqrt(queries.shape[2])
    all_residual = collect(residual, "dp", 0)
    query_latent = jnp.einsum(
        "shn,hnc->shc", queries[:, :, :nope_width], w_absorb, preferred_element_type=jnp.float32
    ).astype(jnp.bfloat16)
    query_full = jnp.concatenate([query_latent, queries[:, :, nope_width:]], axis=2)
    scores = (
        jnp.einsum("shc,slc->shl", query_full, latent_cache, preferred_element_type=jnp.float32)
        * softmax_scale
    )
    positions = lax.broadcasted_iota(jnp.int32, (1, 1, latent_cache.shape[1]), 2)
    scores = jnp.where(positions < lengths[:, None, None], scores, -1e30)
    own_score = (
        jnp.einsum("shc,sc->sh", query_full, new_latent, preferred_element_type=jnp.float32)
        * softmax_scale
    )
    peak = jnp.maximum(jnp.max(scores, axis=2), own_score)
    cached_exp = jnp.exp(scores - peak[:, :, None])
    own_exp = jnp.exp(own_score - peak)
    total = jnp.sum(cached_exp, axis=2) + own_exp
    probs_bf = (cached_exp / total[:, :, None]).astype(jnp.bfloat16)
    own_prob = (own_exp / total).astype(jnp.bfloat16)
    head_latent = jnp.einsum(
        "shl,slc->shc",
        probs_bf,
        latent_cache[:, :, :latent_width],
        preferred_element_type=jnp.float32,
    )
    head_latent = head_latent + own_prob.astype(jnp.float32)[:, :, None] * new_latent[
        :, None, :latent_width
    ].astype(jnp.float32)
    head_latent = head_latent.astype(jnp.bfloat16)
    head_values = jnp.einsum(
        "shc,hcv->shv", head_latent, w_value, preferred_element_type=jnp.float32
    ).astype(jnp.bfloat16)
    head_values = head_values.reshape(sample_rows, -1)
    w_flat = w_out.reshape(w_out.shape[0], -1)
    partial_out = jnp.dot(collect(head_values, "dp", 0), w_flat, preferred_element_type=jnp.float32)
    partial_out = partial_out.reshape(partial_out.shape[0], w_out.shape[1], w_out.shape[2])
    summed_block = sum_at_owner(partial_out.astype(jnp.bfloat16), "hp", 1).astype(jnp.bfloat16)
    attention_out = collect(summed_block, "dp", 2)
    attention_out = attention_out.reshape(attention_out.shape[0], -1)
    hidden_state = all_residual.astype(jnp.float32) + attention_out.astype(jnp.float32)
    row_power = over_copies(jnp.sum(hidden_state * hidden_state, axis=1), "hp") / D
    normed = (
        hidden_state
        * lax.rsqrt(row_power + 1e-06)[:, None]
        * norm_gain.astype(jnp.float32)[None, :]
    ).astype(jnp.bfloat16)
    gate_part = jnp.dot(normed, w_gate, preferred_element_type=jnp.float32)
    up_part = jnp.dot(normed, w_up, preferred_element_type=jnp.float32)
    gate_sum, up_sum = tuple(
        (
            part.astype(jnp.float32)
            for part in side_by_side(
                (gate_part.astype(jnp.bfloat16), up_part.astype(jnp.bfloat16)), "hp", 1, 0
            )
        )
    )
    share_units = (jax.nn.silu(gate_sum) * up_sum).astype(jnp.bfloat16)
    activated = collect(share_units, "hp", 1)
    ffn_out = sum_at_owner(
        jnp.dot(activated, w_down, preferred_element_type=jnp.float32).astype(jnp.bfloat16), "dp", 0
    )
    own_rows = lax.dynamic_slice_in_dim(
        hidden_state, lax.axis_index("dp") * sample_rows, sample_rows, 0
    )
    return (own_rows + ffn_out).astype(jnp.bfloat16)


def solution(mesh):
    in_specs = (
        P("dp", "hp"),
        P("dp", "hp", None),
        P("dp", None, None),
        P("dp", None),
        P("dp"),
        P("hp", None, None),
        P("hp", None, None),
        P("hp", None, "dp"),
        P("hp"),
        P("hp", "dp"),
        P("hp", "dp"),
        P("dp", "hp"),
    )
    out_specs = P("dp", "hp")
    return jax.shard_map(
        on_device, mesh=mesh, in_specs=in_specs, out_specs=out_specs, check_vma=False
    )
```

profile of v0, /device:TPU:0, one launch (start us, length us, event | category | flops | bytes accessed | tf_op | source)
XLA Modules:
  0.0 258.3 jit_solution(3155161711575992530)
XLA Ops:
  6.5 0.0 copy-start
  6.5 1.1 slice.12
  7.6 0.9 slice.13
  8.6 0.7 iota_compare_fusion
  9.3 0.8 slice_convert_fusion
  10.1 0.0 copy-done
  10.1 0.0 copy-start.5
  10.1 0.4 fusion.14
  10.5 0.1 pad_maximum_fusion.1
  10.6 0.3 copy-done.5
  10.9 0.4 fusion.20
  11.2 7.9 %fusion.36 = (f32[32,16]{1,0:T(8,128)S(1)}, f32[32,16,512]{2,1,0:T(8,128)S(1)}) fusion(bf16[32,512,576]{1,2,0:T(8,128)(2,1)} %param.14, bf16[32,16,576]{2,0,1:T(8,128)(2,1)S(1)} %pad_maximum_fusion.1, pred[32,512]{1,0:T(8,128)(4,1)S(1)} %iota_compare_fusion), kind=kOutput, calls=%fused_computation.53 | convolution fusion | flops 302775808 | bytes 20531200 | tf_op jit(solution)/shard_map/shc,slc->shl/dot_general | solution.py:79
  19.2 0.3 fusion.19
  19.5 8.2 %fusion.8 = bf16[32,16,512]{2,1,0:T(8,128)(2,1)S(1)} fusion(bf16[32,512,576]{1,2,0:T(8,128)(2,1)} %param.14, f32[32,16,512]{2,1,0:T(8,128)S(1)} %get-tuple-element.10, f32[32,512]{1,0:T(8,128)S(1)} %slice_convert_fusion, f32[32,16]{1,0:T(8,128)S(1)} %get-tuple-element.8, f32[32,16]{1,0:T(8,128)S(1)} %get-tuple-element.7, f32[32,16]{1,0:T(8,128)S(1)} %multiply_maximum_fusion), kind=kOutput, calls=%fused_computation.15 | convolution fusion | flops 270008320 | bytes 18421760 | tf_op jit(solution)/shard_map/shl,slc->shc/dot_general | solution.py:94
  27.8 2.2 fusion.18
  30.0 0.2 broadcast_in_dim.30
  30.2 0.0 copy-start.8
  30.3 36.3 %all_to_all.36 = bf16[16,32,2048]{2,1,0:T(8,128)(2,1)S(1)} all-to-all(bf16[16,32,2048]{2,1,0:T(8,128)(2,1)S(1)} %broadcast_in_dim.30), channel_id=1, replica_groups=mesh['dp'=16,'hp'=8] {'dp'}, dimensions={0} | all-to-all | bytes 4194304 | tf_op jit(solution)/shard_map/all_to_all | solution.py:13
  66.5 0.0 copy-done.8
  66.5 1.2 fusion.15
  67.7 14.1 %all_to_all.37 = bf16[8,512,1,56]{1,3,2,0:T(8,128)(2,1)S(1)} all-to-all(bf16[8,512,1,56]{1,3,2,0:T(8,128)(2,1)S(1)} %fusion.15), channel_id=1, replica_groups=mesh['dp'=16,'hp'=8] {'hp'}, dimensions={0} | all-to-all | bytes 917504 | tf_op jit(solution)/shard_map/all_to_all | solution.py:35
  81.8 0.0 copy-start.4
  81.8 0.1 reduce_sum.49
  81.8 0.1 broadcast_in_dim.31
  81.9 20.1 %all_to_all.38 = bf16[16,512,1,56]{1,3,2,0:T(8,128)(2,1)S(1)} all-to-all(bf16[16,512,1,56]{1,3,2,0:T(8,128)(2,1)S(1)} %broadcast_in_dim.31), channel_id=1, replica_groups=mesh['dp'=16,'hp'=8] {'dp'}, dimensions={0} | all-to-all | bytes 1835008 | tf_op jit(solution)/shard_map/all_to_all | solution.py:13
  102.0 0.0 copy-done.4
  102.0 0.0 copy-start.6
  102.0 1.0 broadcast_in_dim.26
  103.0 3.6 %all-to-all-start = ((bf16[16,32,896]{2,1,0:T(8,128)(2,1)}), bf16[16,32,896]{2,1,0:T(8,128)(2,1)S(1)}, u32[]{:S(2)}, u32[]{:S(2)}) async-start(bf16[16,32,896]{2,1,0:T(8,128)(2,1)} %broadcast_in_dim.26), calls=%async_computation | async-start | bytes 1835008 | tf_op jit(solution)/shard_map/all_to_all | solution.py:13
  106.6 0.0 copy-done.6
  106.6 2.3 fusion.26
  109.0 2.8 %copy.77 = f32[512,896]{1,0:T(8,128)} copy(f32[512,896]{0,1:T(8,128)} %bitcast.60) | data formatting | bytes 3670016 | tf_op jit(solution)/shard_map/convert_element_type | solution.py:114
  111.7 4.8 %copy.78 = f32[512,1,16,56]{3,2,0,1:T(8,128)} copy(f32[512,1,16,56]{0,3,2,1:T(8,128)} %get-tuple-element.5) | data formatting | bytes 3670016 | tf_op jit(solution)/shard_map/convert_element_type | solution.py:114
  116.6 5.0 %reshape.82 = f32[16,32,896]{2,1,0:T(8,128)} reshape(f32[512,1,16,56]{3,2,0,1:T(8,128)} %copy.78) | data formatting | bytes 3670016 | tf_op jit(solution)/shard_map/convert_element_type | solution.py:114
  121.6 1.6 all-to-all-done
  123.1 1.8 multiply_reduce_fusion
  124.9 0.1 broadcast_in_dim.32
  125.0 0.6 broadcast_in_dim.33
  125.6 3.3 %all-to-all-start.4 = ((f32[8,1,512]{2,1,0:T(1,128)}), f32[8,1,512]{2,1,0:T(1,128)S(1)}, u32[]{:S(2)}, u32[]{:S(2)}) async-start(f32[8,1,512]{2,1,0:T(1,128)} %broadcast_in_dim.33), calls=%async_computation.4 | async-start | bytes 32768 | tf_op jit(solution)/shard_map/all_to_all | solution.py:13
  129.0 0.2 reduce-scatter.4.cloned.1.call-start
  129.2 2.9 %bitcast_add_fusion = f32[512,896]{1,0:T(8,128)} fusion(f32[512,896]{1,0:T(8,128)} %copy.77, bf16[16,32,896]{2,1,0:T(8,128)(2,1)S(1)} %all-to-all-done), kind=kLoop, calls=%fused_computation.7 | loop fusion | flops 917504 | bytes 4587520 | tf_op jit(solution)/shard_map/add | solution.py:114
  132.1 3.0 %all-to-all-done.4 = f32[8,1,512]{2,1,0:T(1,128)S(1)} async-done(((f32[8,1,512]{2,1,0:T(1,128)}), f32[8,1,512]{2,1,0:T(1,128)S(1)}, u32[]{:S(2)}, u32[]{:S(2)}) %all-to-all-start.4) | async-done | bytes 16416 | tf_op jit(solution)/shard_map/all_to_all | solution.py:13
  135.2 0.0 copy-start.2
  135.2 0.0 copy-start.7
  135.2 3.8 %convolution_convert_fusion.1 = bf16[512,1152]{1,0:T(8,128)(2,1)S(1)} fusion(bf16[896,1152]{1,0:T(8,128)(2,1)} %param.21, f32[512,896]{1,0:T(8,128)} %bitcast_add_fusion, f32[896]{0:T(1024)S(1)} %convert_element_type.106, f32[512]{0:T(512)S(1)} %add_rsqrt_fusion), kind=kOutput, calls=%fused_computation.3 | convolution fusion | flops 1058930688 | bytes 5084672 | tf_op jit(solution)/shard_map/dot_general | solution.py:121
  139.0 0.0 copy-done.2
  139.0 0.0 copy-done.7
  139.0 1.6 convolution_convert_fusion
  140.6 1.6 pad_maximum_fusion
  142.2 4.3 %copy.84 = bf16[1024,1152]{0,1:T(8,128)(2,1)} copy(bf16[1024,1152]{1,0:T(8,128)(2,1)} %pad_maximum_fusion) | data formatting | bytes 4718592
  146.5 0.0 reduce-scatter.4.cloned.1.call-update
  146.6 55.9 %reduce-scatter.4.cloned.1.call-done = bf16[144,1024]{1,0:T(8,128)(2,1)} async-done(((bf16[1152,1024]{1,0:T(8,128)(2,1)}), bf16[144,1024]{1,0:T(8,128)(2,1)}) %reduce-scatter.4.cloned.1.call-update) | async-done | bytes 294928
  202.5 1.1 fusion.31
  203.6 0.0 copy-start.3
  203.6 0.1 broadcast_in_dim.60
  203.7 20.3 %all_to_all.39 = bf16[8,512,144]{1,2,0:T(8,128)(2,1)S(1)} all-to-all(bf16[8,512,144]{1,2,0:T(8,128)(2,1)S(1)} %broadcast_in_dim.60), channel_id=1, replica_groups=mesh['dp'=16,'hp'=8] {'hp'}, dimensions={0} | all-to-all | bytes 2359296 | tf_op jit(solution)/shard_map/all_to_all | solution.py:13
  224.0 0.0 copy-done.3
  224.0 0.0 copy-start.1
  224.0 2.5 convolution_convert_fusion.2
  226.4 6.8 %all-to-all-start.6 = ((bf16[16,32,896]{2,1,0:T(8,128)(2,1)}), bf16[16,32,896]{2,1,0:T(8,128)(2,1)S(1)}, u32[]{:S(2)}, u32[]{:S(2)}) async-start(bf16[16,32,896]{2,1,0:T(8,128)(2,1)} %bitcast.62), calls=%async_computation.6 | async-start | bytes 1835008 | tf_op jit(solution)/shard_map/all_to_all | solution.py:35
  233.2 16.5 %all-to-all-done.6 = bf16[16,32,896]{2,1,0:T(8,128)(2,1)S(1)} async-done(((bf16[16,32,896]{2,1,0:T(8,128)(2,1)}), bf16[16,32,896]{2,1,0:T(8,128)(2,1)S(1)}, u32[]{:S(2)}, u32[]{:S(2)}) %all-to-all-start.6) | async-done | bytes 917536 | tf_op jit(solution)/shard_map/all_to_all | solution.py:35
  249.8 0.1 convert_reduce_fusion
  249.9 1.5 add_convert_fusion
  251.4 0.0 copy-done.1
  (7 shorter events, 0.1 us)
Async XLA Ops:
  6.5 3.5 %copy-start = (bf16[16,128,512]{2,1,0:T(8,128)(2,1)S(1)}, bf16[16,128,512]{2,1,0:T(8,128)(2,1)}, u32[]{:S(2)}) copy-start(bf16[16,128,512]{2,1,0:T(8,128)(2,1)} %param.17) | copy-start | bytes 6291460
  10.1 0.8 copy-start.5
  30.2 36.3 %copy-start.8 = (bf16[2048,8,56]{0,2,1:T(8,128)(2,1)S(1)}, bf16[2048,8,56]{0,2,1:T(8,128)(2,1)}, u32[]{:S(2)}) copy-start(bf16[2048,8,56]{0,2,1:T(8,128)(2,1)} %param.19) | copy-start | bytes 5505028
  81.8 20.2 %copy-start.4 = (bf16[32,896]{1,0:T(8,128)(2,1)S(1)}, bf16[32,896]{1,0:T(8,128)(2,1)}, u32[]{:S(2)}) copy-start(bf16[32,896]{1,0:T(8,128)(2,1)} %param.12) | copy-start | bytes 172036
  102.0 4.6 %copy-start.6 = (bf16[896]{0:T(1024)(128)(2,1)S(1)}, bf16[896]{0:T(1024)(128)(2,1)}, u32[]{:S(2)}) copy-start(bf16[896]{0:T(1024)(128)(2,1)} %param.20) | copy-start | bytes 5380
  103.0 20.2 %all-to-all-start = ((bf16[16,32,896]{2,1,0:T(8,128)(2,1)}), bf16[16,32,896]{2,1,0:T(8,128)(2,1)S(1)}, u32[]{:S(2)}, u32[]{:S(2)}) async-start(bf16[16,32,896]{2,1,0:T(8,128)(2,1)} %broadcast_in_dim.26), calls=%async_computation | async-start | bytes 1835008 | tf_op jit(solution)/shard_map/all_to_all | solution.py:13
  125.6 9.5 %all-to-all-start.4 = ((f32[8,1,512]{2,1,0:T(1,128)}), f32[8,1,512]{2,1,0:T(1,128)S(1)}, u32[]{:S(2)}, u32[]{:S(2)}) async-start(f32[8,1,512]{2,1,0:T(1,128)} %broadcast_in_dim.33), calls=%async_computation.4 | async-start | bytes 32768 | tf_op jit(solution)/shard_map/all_to_all | solution.py:13
  129.0 73.5 %reduce-scatter.4.cloned.1.call-start = ((), (), s32[]{:S(2)}) async-start(), calls=%async_computation.8 | async-start | bytes 2654208
  135.2 3.9 %copy-start.2 = (f32[512,896]{1,0:T(8,128)S(1)}, f32[512,896]{1,0:T(8,128)}, u32[]{:S(2)}) copy-start(f32[512,896]{1,0:T(8,128)} %bitcast_add_fusion) | copy-start | bytes 5505028
  135.2 3.9 %copy-start.7 = (bf16[896,1152]{1,0:T(8,128)(2,1)S(1)}, bf16[896,1152]{1,0:T(8,128)(2,1)}, u32[]{:S(2)}) copy-start(bf16[896,1152]{1,0:T(8,128)(2,1)} %param.22) | copy-start | bytes 6193156
  203.6 20.4 %copy-start.3 = (bf16[1152,896]{1,0:T(8,128)(2,1)S(1)}, bf16[1152,896]{1,0:T(8,128)(2,1)}, u32[]{:S(2)}) copy-start(bf16[1152,896]{1,0:T(8,128)(2,1)} %param.23) | copy-start | bytes 6193156
  224.0 27.5 %copy-start.1 = (bf16[16,128,512]{2,1,0:T(8,128)(2,1)S(1)}, bf16[16,128,512]{2,1,0:T(8,128)(2,1)}, u32[]{:S(2)}) copy-start(bf16[16,128,512]{2,1,0:T(8,128)(2,1)} %param.17) | copy-start | bytes 6291460
  226.4 23.4 %all-to-all-start.6 = ((bf16[16,32,896]{2,1,0:T(8,128)(2,1)}), bf16[16,32,896]{2,1,0:T(8,128)(2,1)S(1)}, u32[]{:S(2)}, u32[]{:S(2)}) async-start(bf16[16,32,896]{2,1,0:T(8,128)(2,1)} %bitcast.62), calls=%async_computation.6 | async-start | bytes 1835008 | tf_op jit(solution)/shard_map/all_to_all | solution.py:35
Sparse Core Ops, SparseCore 0:
  146.7 55.7 reduce-scatter.3
where the time goes:
time: 259 us; the launch traced here: 258 us
  blocking collectives  90.7 us (35%)
  waiting for transfers between devices  77 us (30%)
  matrix products  28.2 us (11%)
  local copies, waits for them, and re-layouts  21.3 us (8%)
  starting transfers between devices  14 us (5%)
  between operations  13.6 us (5%)
  other arithmetic  13.4 us (5%)
    all_to_all x3, blocking collectives, from_everyone(): lax.all_to_all(jnp.broadcast_to(x[None], (devices, *x.shape)), axis, 0, 0...  76.6 us
    unnamed x2, waiting for transfers between devices  55.9 us
    all_to_all x1, waiting for transfers between devices, sum_at_owner(): lax.all_to_all(pieces, axis, split_axis=0, concat_axis=0, tiled=True)  16.5 us
    all_to_all x1, blocking collectives, sum_at_owner(): lax.all_to_all(pieces, axis, split_axis=0, concat_axis=0, tiled=True)  14.1 us
    convert_element_type x3, local copies, waits for them, and re-layouts, on_device(): attention_out.astype(jnp.float32)  12.6 us
    dot_general x1, matrix products, on_device(): jnp.einsum('shl,slc->shc', probs_bf, latent_cache[:, :, :latent_width], p...  8.25 us
    dot_general x1, matrix products, on_device(): jnp.einsum('shc,slc->shl', query_full, latent_cache, preferred_element_ty...  7.93 us
    all_to_all x2, starting transfers between devices, from_everyone(): lax.all_to_all(jnp.broadcast_to(x[None], (devices, *x.shape)), axis, 0, 0...  6.97 us
  transfers between devices with their start and end apart: 4, of which 4 were waited for; matrix products, arithmetic and copies ran while one was open for 7% of the time, Pallas kernels for 0%

commit v1 on v0

v1 whole, which is shorter than its diff:
```python
import math

import jax
import jax.numpy as jnp
from jax import lax
from jax.sharding import Mesh, PartitionSpec as P

D = 7168
F32 = jnp.float32
BF16 = jnp.bfloat16
DP = ("x", "h", "c")
CHIPS = ("x", "h")
HP = ("z", "l")


def from_everyone(x, axes):
    devices = lax.axis_size(axes)
    return lax.all_to_all(jnp.broadcast_to(x[None], (devices, *x.shape)), axes, 0, 0, tiled=True)


def exchange(x, axes):
    return lax.all_to_all(x, axes, 0, 0, tiled=True)


def dot(a, b, dims):
    return lax.dot_general(a, b, (dims, ((), ())), preferred_element_type=F32)


def other_core(w):
    return lax.ppermute(w, "c", [(0, 1), (1, 0)])


def attention(queries, latent_cache, new_latent, lengths, w_absorb, w_value):
    nope_width = w_absorb.shape[1]
    latent_width = w_absorb.shape[2]
    softmax_scale = 1.0 / math.sqrt(queries.shape[2])
    query_latent = jnp.einsum(
        "shn,hnc->shc", queries[:, :, :nope_width], w_absorb, preferred_element_type=F32
    ).astype(BF16)
    query_full = jnp.concatenate([query_latent, queries[:, :, nope_width:]], axis=2)
    scores = (
        jnp.einsum("shc,slc->shl", query_full, latent_cache, preferred_element_type=F32)
        * softmax_scale
    )
    positions = lax.broadcasted_iota(jnp.int32, (1, 1, latent_cache.shape[1]), 2)
    scores = jnp.where(positions < lengths[:, None, None], scores, -1e30)
    own_score = (
        jnp.einsum("shc,sc->sh", query_full, new_latent, preferred_element_type=F32)
        * softmax_scale
    )
    peak = jnp.maximum(jnp.max(scores, axis=2), own_score)
    cached_exp = jnp.exp(scores - peak[:, :, None])
    own_exp = jnp.exp(own_score - peak)
    total = jnp.sum(cached_exp, axis=2) + own_exp
    probs_bf = (cached_exp / total[:, :, None]).astype(BF16)
    own_prob = (own_exp / total).astype(BF16)
    head_latent = jnp.einsum(
        "shl,slc->shc", probs_bf, latent_cache[:, :, :latent_width], preferred_element_type=F32
    )
    head_latent = head_latent + own_prob.astype(F32)[:, :, None] * new_latent[
        :, None, :latent_width
    ].astype(F32)
    head_latent = head_latent.astype(BF16)
    head_values = jnp.einsum(
        "shc,hcv->shv", head_latent, w_value, preferred_element_type=F32
    ).astype(BF16)
    return head_values.reshape(queries.shape[0], -1)


def on_device(
    residual,
    queries,
    latent_cache,
    new_latent,
    lengths,
    w_absorb,
    w_value,
    w_out,
    norm_gain,
    w_gate,
    w_up,
    w_down,
):
    rows = queries.shape[0]
    width = residual.shape[1]
    core = lax.axis_index("c")
    chip = lax.axis_index(CHIPS)
    outs = (w_out, other_core(w_out))
    gates = (w_gate, other_core(w_gate))
    ups = (w_up, other_core(w_up))
    downs = (w_down, other_core(w_down))

    residual_rows = from_everyone(residual, CHIPS).reshape(-1, width)
    residual_cols = residual_rows.T

    head_values = attention(queries, latent_cache, new_latent, lengths, w_absorb, w_value)
    all_values = from_everyone(head_values, CHIPS).reshape(-1, head_values.shape[1])
    tokens = all_values.shape[0]

    partial = jnp.stack(
        [
            jnp.einsum("tk,kbf->bft", all_values, w, preferred_element_type=F32).astype(BF16)
            for w in outs
        ],
        axis=1,
    )
    arrived = exchange(partial, HP)
    summed = arrived.astype(F32).sum(axis=0).astype(BF16)
    summed = jnp.where(core == 0, summed, summed[::-1])
    attention_cols = from_everyone(summed, CHIPS).reshape(width, tokens)

    hidden_cols = residual_cols.astype(F32) + attention_cols.astype(F32)
    power_part = jnp.sum(hidden_cols * hidden_cols, axis=0).reshape(lax.axis_size(HP), -1)
    scaled = (hidden_cols * norm_gain.astype(F32)[:, None]).astype(BF16)

    sums = [dot(scaled, w, ((0,), (0,))).astype(BF16) for w in gates + ups]
    both = jnp.concatenate(sums, axis=1)
    both = both.reshape(lax.axis_size(HP), -1, both.shape[1])
    both = exchange(both, HP).astype(F32).sum(axis=0)

    row_power = exchange(power_part, HP).sum(axis=0) / D
    both = both * lax.rsqrt(row_power + 1e-06)[:, None]
    gate_sum, up_sum = jnp.split(both, 2, axis=1)
    share = (jax.nn.silu(gate_sum) * up_sum).astype(BF16)
    activated = from_everyone(share, HP).reshape(tokens, -1)

    units = w_down.shape[0]
    ffn = sum(
        dot(activated[:, i * units : (i + 1) * units], w, ((1,), (0,)))
        for i, w in enumerate(downs)
    ).astype(BF16)
    ffn = exchange(ffn.reshape(-1, rows, width), CHIPS).astype(F32).sum(axis=0)

    pick = (
        lax.broadcasted_iota(jnp.int32, (tokens, rows), 0)
        == lax.broadcasted_iota(jnp.int32, (tokens, rows), 1) + chip * rows
    ).astype(BF16)
    own_attention = dot(pick, attention_cols, ((0,), (1,)))
    own_hidden = residual.astype(F32) + own_attention
    return (own_hidden + ffn).astype(BF16)


def solution(mesh):
    fine = Mesh(mesh.devices.reshape(4, 2, 2, 4, 2), ("x", "h", "c", "z", "l"))
    in_specs = (
        P(DP, HP),
        P(DP, HP, None),
        P(DP, None, None),
        P(DP, None),
        P(DP),
        P(HP, None, None),
        P(HP, None, None),
        P(HP, None, DP),
        P(HP),
        P(HP, DP),
        P(HP, DP),
        P(DP, HP),
    )
    return jax.shard_map(
        on_device, mesh=fine, in_specs=in_specs, out_specs=P(DP, HP), check_vma=False
    )
```

time: 259 us -> 185 us (0.71)
  blocking collectives: 90.7 us -> 42.2 us
  waiting for transfers between devices: 77 us -> 59.4 us
  starting transfers between devices: 14 us -> 30.4 us
  local copies, waits for them, and re-layouts: 21.3 us -> 6.61 us
  between operations: 13.6 us -> 0.34 us
  matrix products: 28.2 us -> 36.1 us
  other arithmetic: 13.4 us -> 8.54 us
    unnamed x2 -> x0, waiting for transfers between devices: 55.9 us -> none
    all_to_all x4 -> x2, blocking collectives: 90.7 us -> 42.2 us  [from_everyone(): lax.all_to_all(jnp.broadcast_to(x[None], (devices, *x.shape)), axes, 0, 0...]
    all_to_all x3 -> x6, waiting for transfers between devices: 21.1 us -> 59.4 us  [the longest x4 43.2 us: exchange(): return lax.all_to_all(x, axes, 0, 0, tiled=True)]
    all_to_all x3 -> x6, starting transfers between devices: 13.8 us -> 29.9 us  [the longest x4 22.3 us: exchange(): return lax.all_to_all(x, axes, 0, 0, tiled=True)]
    convert_element_type x3 -> x1, local copies, waits for them, and re-layouts: 12.6 us -> 1.22 us  [on_device(): hidden_cols = residual_cols.astype(F32) + attention_cols.astype(F32)]
    dot_general x9 -> x12, matrix products: 28.2 us -> 33.2 us  [the longest x7 13.2 us: dot(): return lax.dot_general(a, b, (dims, ((), ())), preferred_element_type=F32)]
    unnamed x20 -> x17, local copies, waits for them, and re-layouts: 4.65 us -> 0.08 us
    convert_element_type x5 -> x4, other arithmetic: 5.73 us -> 2 us  [the longest x1 1.08 us: on_device(): hidden_cols = residual_cols.astype(F32) + attention_cols.astype(F32)]
  transfers between devices with their start and end apart: 4 -> 10, of which waited for: 4 -> 5; matrix products, arithmetic and copies ran while one was open for 7% -> 24% of each run, Pallas kernels for 0% -> 0%
where the time goes in v1:
time: 185 us; the launch traced here: 184 us
  waiting for transfers between devices  59.4 us (32%)
  blocking collectives  42.2 us (23%)
  matrix products  36.1 us (20%)
  starting transfers between devices  30.4 us (16%)
  other arithmetic  8.54 us (5%)
  local copies, waits for them, and re-layouts  6.61 us (4%)
    all_to_all x4, waiting for transfers between devices, exchange(): return lax.all_to_all(x, axes, 0, 0, tiled=True)  43.2 us
    all_to_all x2, blocking collectives, from_everyone(): lax.all_to_all(jnp.broadcast_to(x[None], (devices, *x.shape)), axes, 0, 0...  42.2 us
    all_to_all x4, starting transfers between devices, exchange(): return lax.all_to_all(x, axes, 0, 0, tiled=True)  22.3 us
    all_to_all x2, waiting for transfers between devices, from_everyone(): lax.all_to_all(jnp.broadcast_to(x[None], (devices, *x.shape)), axes, 0, 0...  16.2 us
    dot_general x7, matrix products, dot(): return lax.dot_general(a, b, (dims, ((), ())), preferred_element_type=F32)  13.2 us
    dot_general x1, matrix products, attention(): jnp.einsum('shl,slc->shc', probs_bf, latent_cache[:, :, :latent_width], p...  9.04 us
    dot_general x1, matrix products, attention(): jnp.einsum('shc,slc->shl', query_full, latent_cache, preferred_element_ty...  7.92 us
    all_to_all x2, starting transfers between devices, from_everyone(): lax.all_to_all(jnp.broadcast_to(x[None], (devices, *x.shape)), axes, 0, 0...  7.61 us
  transfers between devices with their start and end apart: 10, of which 5 were waited for; matrix products, arithmetic and copies ran while one was open for 24% of the time, Pallas kernels for 0%

profile of v1, /device:TPU:0, one launch (start us, length us, event | category | flops | bytes accessed | tf_op | source)
XLA Modules:
  0.0 183.6 jit_solution(7597241419474969996)
XLA Ops:
  0.0 0.0 copy-start
  0.0 0.0 collective-permute-start
  0.0 1.1 slice.18
  1.1 0.9 slice.19
  2.0 0.7 iota_compare_fusion.1
  2.8 0.0 copy-start.6
  2.8 0.8 slice_convert_fusion
  3.6 0.0 copy-done
  3.6 0.4 fusion.10
  4.0 0.1 pad_maximum_fusion.1
  4.1 0.4 fusion.18
  4.5 7.9 %fusion.32 = (f32[32,16]{1,0:T(8,128)S(1)}, f32[32,16,512]{2,1,0:T(8,128)S(1)}) fusion(bf16[32,512,576]{1,2,0:T(8,128)(2,1)} %param.14, bf16[32,16,576]{2,0,1:T(8,128)(2,1)S(1)} %pad_maximum_fusion.1, pred[32,512]{1,0:T(8,128)(4,1)S(1)} %iota_compare_fusion.1), kind=kOutput, calls=%fused_computation.61 | convolution fusion | flops 302775808 | bytes 20531200 | tf_op jit(solution)/shard_map/shc,slc->shl/dot_general | solution.py:42
  12.4 0.3 fusion.14
  12.7 9.0 %fusion.6 = bf16[32,16,512]{2,1,0:T(8,128)(2,1)} fusion(bf16[32,512,576]{1,2,0:T(8,128)(2,1)} %param.14, f32[32,16,512]{2,1,0:T(8,128)S(1)} %get-tuple-element.10, f32[32,512]{1,0:T(8,128)S(1)} %slice_convert_fusion, f32[32,16]{1,0:T(8,128)S(1)} %get-tuple-element.8, f32[32,16]{1,0:T(8,128)S(1)} %get-tuple-element.7, f32[32,16]{1,0:T(8,128)S(1)} %multiply_maximum_fusion), kind=kOutput, calls=%fused_computation.12 | convolution fusion | flops 270008320 | bytes 18421760 | tf_op jit(solution)/shard_map/shl,slc->shc/dot_general | solution.py:57
  21.8 2.4 %fusion.11 = bf16[16,4,8,128]{3,2,1,0:T(8,128)(2,1)S(1)} fusion(bf16[16,512,128]{2,1,0:T(8,128)(2,1)} %param.18, bf16[32,16,512]{2,1,0:T(8,128)(2,1)} %fusion.6), kind=kOutput, calls=%fused_computation.17 | convolution fusion | flops 67174400 | bytes 2752512 | tf_op jit(solution)/shard_map/shc,hcv->shv/dot_general | solution.py:64
  24.1 0.0 copy-start.3
  24.2 0.1 broadcast_in_dim.25
  24.3 24.3 %all_to_all.44 = bf16[8,32,2048]{2,1,0:T(8,128)(2,1)S(1)} all-to-all(bf16[8,32,2048]{2,1,0:T(8,128)(2,1)S(1)} %broadcast_in_dim.25), channel_id=1, replica_groups=mesh['x'=4,'h'=2,'c'=2,'z'=4,'l'=2] {'x','h'}, dimensions={0} | all-to-all | bytes 2097152 | tf_op jit(solution)/shard_map/all_to_all | solution.py:18
  48.7 0.7 fusion.33
  49.3 0.0 collective-permute-done
  49.3 2.2 %fusion.34 = f32[256,448]{0,1:S(1)} fusion(bf16[256,2048]{1,0:T(8,128)(2,1)S(1)} %bitcast.59, bf16[2048,448]{0,1:T(8,128)(2,1)} %bitcast.10), kind=kOutput, calls=%fused_computation.63 | convolution fusion | flops 469762048 | bytes 3342336
  51.5 0.0 copy-start.5
  51.6 0.8 copy.52
  52.5 5.6 %all-to-all-start.1 = ((bf16[8,2,56,256]{3,2,1,0:T(8,128)(2,1)}), bf16[8,2,56,256]{3,2,1,0:T(8,128)(2,1)S(1)}, u32[]{:S(2)}, u32[]{:S(2)}) async-start(bf16[8,2,56,256]{3,2,1,0:T(8,128)(2,1)} %copy.52), calls=%async_computation.1 | async-start | bytes 917504 | tf_op jit(solution)/shard_map/all_to_all | solution.py:22
  58.0 0.0 collective-permute-start.2
  58.0 0.5 collective-permute-start.1
  58.5 7.9 %all-to-all-done.1 = bf16[8,2,56,256]{3,2,1,0:T(8,128)(2,1)S(1)} async-done(((bf16[8,2,56,256]{3,2,1,0:T(8,128)(2,1)}), bf16[8,2,56,256]{3,2,1,0:T(8,128)(2,1)S(1)}, u32[]{:S(2)}, u32[]{:S(2)}) %all-to-all-start.1) | async-done | bytes 458784 | tf_op jit(solution)/shard_map/all_to_all | solution.py:22
  66.4 0.8 broadcast_in_dim.27
  67.2 4.1 %all-to-all-start.3 = ((bf16[8,32,896]{2,1,0:T(8,128)(2,1)}), bf16[8,32,896]{2,1,0:T(8,128)(2,1)S(1)}, u32[]{:S(2)}, u32[]{:S(2)}) async-start(bf16[8,32,896]{2,1,0:T(8,128)(2,1)} %broadcast_in_dim.27), calls=%async_computation.3 | async-start | bytes 917504 | tf_op jit(solution)/shard_map/all_to_all | solution.py:18
  71.4 0.1 reduce_sum.58
  71.4 9.4 %all-to-all-done.3 = bf16[8,32,896]{2,1,0:T(8,128)(2,1)S(1)} async-done(((bf16[8,32,896]{2,1,0:T(8,128)(2,1)}), bf16[8,32,896]{2,1,0:T(8,128)(2,1)S(1)}, u32[]{:S(2)}, u32[]{:S(2)}) %all-to-all-start.3) | async-done | bytes 458784 | tf_op jit(solution)/shard_map/all_to_all | solution.py:18
  80.9 0.8 broadcast_in_dim.26
  81.7 3.5 %all-to-all-start.2 = ((bf16[8,2,56,256]{3,2,1,0:T(8,128)(2,1)}), bf16[8,2,56,256]{3,2,1,0:T(8,128)(2,1)S(1)}, u32[]{:S(2)}, u32[]{:S(2)}) async-start(bf16[8,2,56,256]{3,2,1,0:T(8,128)(2,1)} %broadcast_in_dim.26), calls=%async_computation.2 | async-start | bytes 917504 | tf_op jit(solution)/shard_map/all_to_all | solution.py:18
  85.2 1.1 bitcast_convert_fusion
  86.3 1.2 copy.53
  87.5 6.8 %all-to-all-done.2 = bf16[8,2,56,256]{3,2,1,0:T(8,128)(2,1)S(1)} async-done(((bf16[8,2,56,256]{3,2,1,0:T(8,128)(2,1)}), bf16[8,2,56,256]{3,2,1,0:T(8,128)(2,1)S(1)}, u32[]{:S(2)}, u32[]{:S(2)}) %all-to-all-start.2) | async-done | bytes 458784 | tf_op jit(solution)/shard_map/all_to_all | solution.py:18
  94.3 1.4 multiply_reduce_fusion
  95.7 0.7 all_to_all.32
  96.4 3.3 %all-to-all-start.5 = ((f32[8,1,32]{2,1,0:T(1,128)}), f32[8,1,32]{2,1,0:T(1,128)S(1)}, u32[]{:S(2)}, u32[]{:S(2)}) async-start(f32[8,1,32]{2,1,0:T(1,128)} %all_to_all.32), calls=%async_computation.5 | async-start | bytes 8192 | tf_op jit(solution)/shard_map/all_to_all | solution.py:22
  99.7 0.0 copy-start.2
  99.7 2.6 %convolution_convert_fusion.1 = bf16[256,1152]{1,0:T(8,128)(2,1)S(1)} fusion(bf16[896,256]{1,0:T(8,128)(2,1)S(1)} %get-tuple-element.6, bf16[896,1152]{1,0:T(8,128)(2,1)} %param.22), kind=kOutput, calls=%fused_computation.4 | convolution fusion | flops 528777216 | bytes 3112960 | tf_op jit(solution)/shard_map/dot_general | solution.py:26
  102.3 0.9 convolution_convert_fusion.3
  103.2 0.0 collective-permute-done.2
  103.2 2.4 %convolution_convert_fusion = bf16[256,1152]{1,0:T(8,128)(2,1)S(1)} fusion(bf16[896,256]{1,0:T(8,128)(2,1)S(1)} %get-tuple-element.6, bf16[896,1152]{1,0:T(8,128)(2,1)} %collective-permute-done.2), kind=kOutput, calls=%fused_computation.3 | convolution fusion | flops 528777216 | bytes 3112960 | tf_op jit(solution)/shard_map/dot_general | solution.py:26
  105.7 0.0 collective-permute-done.1
  105.7 2.4 %convolution_convert_fusion.2 = bf16[256,1152]{1,0:T(8,128)(2,1)S(1)} fusion(bf16[896,256]{1,0:T(8,128)(2,1)S(1)} %get-tuple-element.6, bf16[896,1152]{1,0:T(8,128)(2,1)} %collective-permute-done.1), kind=kOutput, calls=%fused_computation.5 | convolution fusion | flops 528777216 | bytes 3112960 | tf_op jit(solution)/shard_map/dot_general | solution.py:26
  108.1 1.6 pad_maximum_fusion
  109.7 0.0 all-to-all-done.5
  109.7 5.6 %all-to-all-start.4 = ((bf16[8,32,4608]{2,1,0:T(8,128)(2,1)}), bf16[8,32,4608]{2,1,0:T(8,128)(2,1)}, u32[]{:S(2)}, u32[]{:S(2)}) async-start(bf16[8,32,4608]{2,1,0:T(8,128)(2,1)} %bitcast.60), calls=%async_computation.4 | async-start | bytes 4718592 | tf_op jit(solution)/shard_map/all_to_all | solution.py:22
  115.3 0.0 collective-permute-start.3
  115.3 25.9 %all-to-all-done.4 = bf16[8,32,4608]{2,1,0:T(8,128)(2,1)} async-done(((bf16[8,32,4608]{2,1,0:T(8,128)(2,1)}), bf16[8,32,4608]{2,1,0:T(8,128)(2,1)}, u32[]{:S(2)}, u32[]{:S(2)}) %all-to-all-start.4) | async-done | bytes 2359328 | tf_op jit(solution)/shard_map/all_to_all | solution.py:22
  141.2 2.1 %convert_reduce_fusion = f32[32,4608]{1,0:T(8,128)S(1)} fusion(bf16[8,32,4608]{2,1,0:T(8,128)(2,1)} %all-to-all-done.4), kind=kLoop, calls=%fused_computation.2 | loop fusion | flops 2211840 | bytes 2949120 | tf_op jit(solution)/shard_map/reduce_sum | solution.py:119
  143.3 0.1 broadcast_multiply_fusion
  143.4 0.0 copy-start.1
  143.4 0.1 fusion.24
  143.5 0.1 broadcast_in_dim.28
  143.6 17.9 %all_to_all.45 = bf16[8,32,2304]{2,1,0:T(8,128)(2,1)S(1)} all-to-all(bf16[8,32,2304]{2,1,0:T(8,128)(2,1)S(1)} %broadcast_in_dim.28), channel_id=1, replica_groups=mesh['x'=4,'h'=2,'c'=2,'z'=4,'l'=2] {'z','l'}, dimensions={0} | all-to-all | bytes 2359296 | tf_op jit(solution)/shard_map/all_to_all | solution.py:18
  161.5 0.8 fusion.16
  162.3 0.0 collective-permute-done.3
  162.3 3.2 %fusion.9 = bf16[256,896]{1,0:T(8,128)(2,1)} fusion(f32[256,896]{1,0:T(8,128)S(1)} %fusion.16, bf16[1152,896]{1,0:T(8,128)(2,1)} %collective-permute-done.3, bf16[256,2304]{1,0:T(8,128)(2,1)S(1)} %bitcast.62), kind=kOutput, calls=%fused_computation.14 | convolution fusion | flops 528941056 | bytes 4030464 | tf_op jit(solution)/shard_map/dot_general | solution.py:26
  165.5 7.8 %all-to-all-start.7 = ((bf16[8,32,896]{2,1,0:T(8,128)(2,1)}), bf16[8,32,896]{2,1,0:T(8,128)(2,1)S(1)}, u32[]{:S(2)}, u32[]{:S(2)}) async-start(bf16[8,32,896]{2,1,0:T(8,128)(2,1)} %bitcast.20), calls=%async_computation.7 | async-start | bytes 917504 | tf_op jit(solution)/shard_map/all_to_all | solution.py:22
  173.3 9.4 %all-to-all-done.7 = bf16[8,32,896]{2,1,0:T(8,128)(2,1)S(1)} async-done(((bf16[8,32,896]{2,1,0:T(8,128)(2,1)}), bf16[8,32,896]{2,1,0:T(8,128)(2,1)S(1)}, u32[]{:S(2)}, u32[]{:S(2)}) %all-to-all-start.7) | async-done | bytes 458784 | tf_op jit(solution)/shard_map/all_to_all | solution.py:22
  182.7 0.1 convert_reduce_fusion.1
  182.7 0.9 fusion.13
  (20 shorter events, 0.2 us)
Async XLA Ops:
  0.0 3.6 %copy-start = (bf16[16,128,512]{2,1,0:T(8,128)(2,1)S(1)}, bf16[16,128,512]{2,1,0:T(8,128)(2,1)}, u32[]{:S(2)}) copy-start(bf16[16,128,512]{2,1,0:T(8,128)(2,1)} %param.17) | copy-start | bytes 6291460
  0.0 49.3 %collective-permute-start = (bf16[2048,8,56]{0,2,1:T(8,128)(2,1)}, bf16[2048,8,56]{0,2,1:T(8,128)(2,1)}, u32[]{:S(2)}, u32[]{:S(2)}) collective-permute-start(bf16[2048,8,56]{0,2,1:T(8,128)(2,1)} %param.19), channel_id=1, source_target_pairs={{0,8},{8,0},{1,9},{9,1},{2,10},{10,2},{3,11},{11,3},{4,12},{12,4},... | collective-permute-start | bytes 5505032 | tf_op jit(solution)/shard_map/ppermute | solution.py:30
  2.8 1.3 copy-start.6
  24.1 24.5 %copy-start.3 = (bf16[2048,8,56]{0,2,1:T(8,128)(2,1)S(1)}, bf16[2048,8,56]{0,2,1:T(8,128)(2,1)}, u32[]{:S(2)}) copy-start(bf16[2048,8,56]{0,2,1:T(8,128)(2,1)} %param.19) | copy-start | bytes 5505028
  51.5 14.9 %copy-start.5 = (bf16[32,896]{1,0:T(8,128)(2,1)S(1)}, bf16[32,896]{1,0:T(8,128)(2,1)}, u32[]{:S(2)}) copy-start(bf16[32,896]{1,0:T(8,128)(2,1)} %param.12) | copy-start | bytes 172036
  52.4 32.7 %copy-start.7 = (bf16[896]{0:T(1024)(128)(2,1)S(1)}, bf16[896]{0:T(1024)(128)(2,1)}, u32[]{:S(2)}) copy-start(bf16[896]{0:T(1024)(128)(2,1)} %param.20) | copy-start | bytes 5380
  52.5 14.0 %all-to-all-start.1 = ((bf16[8,2,56,256]{3,2,1,0:T(8,128)(2,1)}), bf16[8,2,56,256]{3,2,1,0:T(8,128)(2,1)S(1)}, u32[]{:S(2)}, u32[]{:S(2)}) async-start(bf16[8,2,56,256]{3,2,1,0:T(8,128)(2,1)} %copy.52), calls=%async_computation.1 | async-start | bytes 917504 | tf_op jit(solution)/shard_map/all_to_all | solution.py:22
  58.0 45.2 %collective-permute-start.2 = (bf16[896,1152]{1,0:T(8,128)(2,1)}, bf16[896,1152]{1,0:T(8,128)(2,1)}, u32[]{:S(2)}, u32[]{:S(2)}) collective-permute-start(bf16[896,1152]{1,0:T(8,128)(2,1)} %param.22), channel_id=1, source_target_pairs={{0,8},{8,0},{1,9},{9,1},{2,10},{10,2},{3,11},{11,3},{4,12},{12,4},... | collective-permute-start | bytes 6193160 | tf_op jit(solution)/shard_map/ppermute | solution.py:30
  58.0 47.6 %collective-permute-start.1 = (bf16[896,1152]{1,0:T(8,128)(2,1)}, bf16[896,1152]{1,0:T(8,128)(2,1)}, u32[]{:S(2)}, u32[]{:S(2)}) collective-permute-start(bf16[896,1152]{1,0:T(8,128)(2,1)} %param.21), channel_id=1, source_target_pairs={{0,8},{8,0},{1,9},{9,1},{2,10},{10,2},{3,11},{11,3},{4,12},{12,4},... | collective-permute-start | bytes 6193160 | tf_op jit(solution)/shard_map/ppermute | solution.py:30
  67.2 13.6 %all-to-all-start.3 = ((bf16[8,32,896]{2,1,0:T(8,128)(2,1)}), bf16[8,32,896]{2,1,0:T(8,128)(2,1)S(1)}, u32[]{:S(2)}, u32[]{:S(2)}) async-start(bf16[8,32,896]{2,1,0:T(8,128)(2,1)} %broadcast_in_dim.27), calls=%async_computation.3 | async-start | bytes 917504 | tf_op jit(solution)/shard_map/all_to_all | solution.py:18
  80.9 4.3 %copy-start.4 = (bf16[8,32,896]{2,1,0:T(8,128)(2,1)}, bf16[8,32,896]{2,1,0:T(8,128)(2,1)S(1)}, u32[]{:S(2)}) copy-start(bf16[8,32,896]{2,1,0:T(8,128)(2,1)S(1)} %all-to-all-done.3) | copy-start | bytes 1376260
  81.7 12.6 %all-to-all-start.2 = ((bf16[8,2,56,256]{3,2,1,0:T(8,128)(2,1)}), bf16[8,2,56,256]{3,2,1,0:T(8,128)(2,1)S(1)}, u32[]{:S(2)}, u32[]{:S(2)}) async-start(bf16[8,2,56,256]{3,2,1,0:T(8,128)(2,1)} %broadcast_in_dim.26), calls=%async_computation.2 | async-start | bytes 917504 | tf_op jit(solution)/shard_map/all_to_all | solution.py:18
  96.4 13.3 %all-to-all-start.5 = ((f32[8,1,32]{2,1,0:T(1,128)}), f32[8,1,32]{2,1,0:T(1,128)S(1)}, u32[]{:S(2)}, u32[]{:S(2)}) async-start(f32[8,1,32]{2,1,0:T(1,128)} %all_to_all.32), calls=%async_computation.5 | async-start | bytes 8192 | tf_op jit(solution)/shard_map/all_to_all | solution.py:22
  99.7 2.6 %copy-start.2 = (bf16[896,1152]{1,0:T(8,128)(2,1)S(1)}, bf16[896,1152]{1,0:T(8,128)(2,1)}, u32[]{:S(2)}) copy-start(bf16[896,1152]{1,0:T(8,128)(2,1)} %param.21) | copy-start | bytes 6193156
  109.7 31.5 %all-to-all-start.4 = ((bf16[8,32,4608]{2,1,0:T(8,128)(2,1)}), bf16[8,32,4608]{2,1,0:T(8,128)(2,1)}, u32[]{:S(2)}, u32[]{:S(2)}) async-start(bf16[8,32,4608]{2,1,0:T(8,128)(2,1)} %bitcast.60), calls=%async_computation.4 | async-start | bytes 4718592 | tf_op jit(solution)/shard_map/all_to_all | solution.py:22
  115.3 47.0 %collective-permute-start.3 = (bf16[1152,896]{1,0:T(8,128)(2,1)}, bf16[1152,896]{1,0:T(8,128)(2,1)}, u32[]{:S(2)}, u32[]{:S(2)}) collective-permute-start(bf16[1152,896]{1,0:T(8,128)(2,1)} %param.23), channel_id=1, source_target_pairs={{0,8},{8,0},{1,9},{9,1},{2,10},{10,2},{3,11},{11,3},{4,12},{12,4},... | collective-permute-start | bytes 6193160 | tf_op jit(solution)/shard_map/ppermute | solution.py:30
  143.4 18.1 %copy-start.1 = (bf16[1152,896]{1,0:T(8,128)(2,1)S(1)}, bf16[1152,896]{1,0:T(8,128)(2,1)}, u32[]{:S(2)}) copy-start(bf16[1152,896]{1,0:T(8,128)(2,1)} %param.23) | copy-start | bytes 6193156
  165.5 17.2 %all-to-all-start.7 = ((bf16[8,32,896]{2,1,0:T(8,128)(2,1)}), bf16[8,32,896]{2,1,0:T(8,128)(2,1)S(1)}, u32[]{:S(2)}, u32[]{:S(2)}) async-start(bf16[8,32,896]{2,1,0:T(8,128)(2,1)} %bitcast.20), calls=%async_computation.7 | async-start | bytes 917504 | tf_op jit(solution)/shard_map/all_to_all | solution.py:22

commit v2 on v1

--- a/solution.py
+++ b/solution.py
@@ -3,9 +3,13 @@
 import jax
 import jax.numpy as jnp
 from jax import lax
+from jax.experimental import pallas as pl
+from jax.experimental.pallas import tpu as pltpu
 from jax.sharding import Mesh, PartitionSpec as P
 
+
 D = 7168
+LANES = 128
 F32 = jnp.float32
 BF16 = jnp.bfloat16
 DP = ("x", "h", "c")
@@ -30,7 +34,102 @@
     return lax.ppermute(w, "c", [(0, 1), (1, 0)])
 
 
-def attention(queries, latent_cache, new_latent, lengths, w_absorb, w_value):
+VMEM = pl.BlockSpec(memory_space=pltpu.VMEM)
+HBM = pl.BlockSpec(memory_space=pl.ANY)
+
+
+def fetch(sources, slots, sems):
+    copies = [
+        pltpu.make_async_copy(source, slots.at[i], sems.at[i]) for i, source in enumerate(sources)
+    ]
+    for copy in copies:
+        copy.start()
+    return copies
+
+
+def fetch_scratch(sources):
+    return [
+        pltpu.VMEM((len(sources), *sources[0].shape), sources[0].dtype),
+        pltpu.SemaphoreType.DMA((len(sources),)),
+    ]
+
+
+def project(values, weights):
+    inner, blocks, cols = weights[0].shape
+    rows = values.shape[0]
+    weights = [w.transpose(1, 2, 0).reshape(blocks * cols, inner) for w in weights]
+
+    def kernel(values, *refs):
+        sources, (out, slots, sems) = refs[: len(weights)], refs[len(weights) :]
+        for i, copy in enumerate(fetch(sources, slots, sems)):
+            copy.wait()
+            part = dot(slots[i], values[...], ((1,), (1,))).astype(BF16)
+            for b in range(blocks):
+                out[b, i] = part[b * cols : (b + 1) * cols]
+
+    return pl.pallas_call(
+        kernel,
+        in_specs=[VMEM] + [HBM] * len(weights),
+        out_specs=VMEM,
+        out_shape=jax.ShapeDtypeStruct((blocks, len(weights), cols, rows), BF16),
+        scratch_shapes=fetch_scratch(weights),
+        name="project",
+    )(values, *weights)
+
+
+def expand(residual_cols, attention_cols, gain, weights):
+    _, tokens = attention_cols.shape
+    units = weights[0].shape[1]
+
+    def kernel(residual, attention_out, gain, *refs):
+        sources, (out, slots, sems) = refs[: len(weights)], refs[len(weights) :]
+        copies = fetch(sources, slots, sems)
+        hidden = (residual[...].astype(F32) + attention_out[...].astype(F32)).T
+        power = jnp.sum(hidden * hidden, axis=1, keepdims=True)
+        high = power.astype(BF16).astype(F32)
+        middle = (power - high).astype(BF16).astype(F32)
+        low = power - high - middle
+        lane = lax.broadcasted_iota(jnp.int32, (tokens, LANES), 1)
+        parts = jnp.where(lane == 0, high, jnp.where(lane == 1, middle, low))
+        out[:, len(weights) * units :] = jnp.where(lane < 3, parts, 0.0).astype(BF16)
+        scaled = (hidden * gain[...]).astype(BF16)
+        for i, copy in enumerate(copies):
+            copy.wait()
+            out[:, i * units : (i + 1) * units] = dot(scaled, slots[i], ((1,), (0,))).astype(BF16)
+
+    return pl.pallas_call(
+        kernel,
+        in_specs=[VMEM] * 3 + [HBM] * len(weights),
+        out_specs=VMEM,
+        out_shape=jax.ShapeDtypeStruct((tokens, len(weights) * units + LANES), BF16),
+        scratch_shapes=fetch_scratch(weights),
+        name="expand",
+    )(residual_cols, attention_cols, gain, *weights)
+
+
+def contract(activated, weights):
+    units, width = weights[0].shape
+
+    def kernel(activated, *refs):
+        sources, (out, slots, sems) = refs[: len(weights)], refs[len(weights) :]
+        total = None
+        for i, copy in enumerate(fetch(sources, slots, sems)):
+            copy.wait()
+            part = dot(activated[:, i * units : (i + 1) * units], slots[i], ((1,), (0,)))
+            total = part if total is None else total + part
+        out[...] = total.astype(BF16)
+
+    return pl.pallas_call(
+        kernel,
+        in_specs=[VMEM] + [HBM] * len(weights),
+        out_specs=VMEM,
+        out_shape=jax.ShapeDtypeStruct((activated.shape[0], width), BF16),
+        scratch_shapes=fetch_scratch(weights),
+        name="contract",
+    )(activated, *weights)
+
+
+def attention(queries, latent_cache, new_latent, lengths, w_absorb):
     nope_width = w_absorb.shape[1]
     latent_width = w_absorb.shape[2]
     softmax_scale = 1.0 / math.sqrt(queries.shape[2])
@@ -60,14 +159,10 @@
     head_latent = head_latent + own_prob.astype(F32)[:, :, None] * new_latent[
         :, None, :latent_width
     ].astype(F32)
-    head_latent = head_latent.astype(BF16)
-    head_values = jnp.einsum(
-        "shc,hcv->shv", head_latent, w_value, preferred_element_type=F32
-    ).astype(BF16)
-    return head_values.reshape(queries.shape[0], -1)
-
-
-def on_device(
+    return head_latent.astype(BF16)
+
+
+def layer(
     residual,
     queries,
     latent_cache,
@@ -85,50 +180,48 @@
     width = residual.shape[1]
     core = lax.axis_index("c")
     chip = lax.axis_index(CHIPS)
-    outs = (w_out, other_core(w_out))
-    gates = (w_gate, other_core(w_gate))
-    ups = (w_up, other_core(w_up))
-    downs = (w_down, other_core(w_down))
-
+    w_out_other = other_core(w_out)
+    w_gate_other = other_core(w_gate)
+    w_up_other = other_core(w_up)
+    w_down_other = other_core(w_down)
     residual_rows = from_everyone(residual, CHIPS).reshape(-1, width)
+
+    head_latent = attention(queries, latent_cache, new_latent, lengths, w_absorb)
+    head_latent, residual_rows, w_out_other = lax.optimization_barrier(
+        (head_latent, residual_rows, w_out_other)
+    )
+    head_values = jnp.einsum("shc,hcv->shv", head_latent, w_value, preferred_element_type=F32)
+    head_values = head_values.astype(BF16).reshape(rows, -1)
+    all_values = from_everyone(head_values, CHIPS).reshape(-1, head_values.shape[1])
     residual_cols = residual_rows.T
-
-    head_values = attention(queries, latent_cache, new_latent, lengths, w_absorb, w_value)
-    all_values = from_everyone(head_values, CHIPS).reshape(-1, head_values.shape[1])
+    all_values, residual_cols, w_gate_other, w_up_other, w_down_other = lax.optimization_barrier(
+        (all_values, residual_cols, w_gate_other, w_up_other, w_down_other)
+    )
     tokens = all_values.shape[0]
 
-    partial = jnp.stack(
-        [
-            jnp.einsum("tk,kbf->bft", all_values, w, preferred_element_type=F32).astype(BF16)
-            for w in outs
-        ],
-        axis=1,
-    )
+    partial = project(all_values, (w_out, w_out_other))
     arrived = exchange(partial, HP)
     summed = arrived.astype(F32).sum(axis=0).astype(BF16)
     summed = jnp.where(core == 0, summed, summed[::-1])
     attention_cols = from_everyone(summed, CHIPS).reshape(width, tokens)
 
-    hidden_cols = residual_cols.astype(F32) + attention_cols.astype(F32)
-    power_part = jnp.sum(hidden_cols * hidden_cols, axis=0).reshape(lax.axis_size(HP), -1)
-    scaled = (hidden_cols * norm_gain.astype(F32)[:, None]).astype(BF16)
-
-    sums = [dot(scaled, w, ((0,), (0,))).astype(BF16) for w in gates + ups]
-    both = jnp.concatenate(sums, axis=1)
-    both = both.reshape(lax.axis_size(HP), -1, both.shape[1])
-    both = exchange(both, HP).astype(F32).sum(axis=0)
-
-    row_power = exchange(power_part, HP).sum(axis=0) / D
-    both = both * lax.rsqrt(row_power + 1e-06)[:, None]
-    gate_sum, up_sum = jnp.split(both, 2, axis=1)
+    both = expand(
+        residual_cols,
+        attention_cols,
+        norm_gain.astype(F32)[None, :],
+        (w_gate, w_gate_other, w_up, w_up_other),
+    )
+    both = exchange(both.reshape(lax.axis_size(HP), -1, both.shape[1]), HP)
+    both = both.astype(F32).sum(axis=0)
+    units = both.shape[1] // 2 - LANES // 2
+    row_power = jnp.sum(both[:, 2 * units :], axis=1, keepdims=True) / D
+    factor = lax.rsqrt(row_power + 1e-06)
+    gate_sum = both[:, :units] * factor
+    up_sum = both[:, units : 2 * units] * factor
     share = (jax.nn.silu(gate_sum) * up_sum).astype(BF16)
     activated = from_everyone(share, HP).reshape(tokens, -1)
 
-    units = w_down.shape[0]
-    ffn = sum(
-        dot(activated[:, i * units : (i + 1) * units], w, ((1,), (0,)))
-        for i, w in enumerate(downs)
-    ).astype(BF16)
+    ffn = contract(activated, (w_down, w_down_other))
     ffn = exchange(ffn.reshape(-1, rows, width), CHIPS).astype(F32).sum(axis=0)
 
     pick = (
@@ -156,6 +249,4 @@
         P(HP, DP),
         P(DP, HP),
     )
-    return jax.shard_map(
-        on_device, mesh=fine, in_specs=in_specs, out_specs=P(DP, HP), check_vma=False
-    )
+    return jax.shard_map(layer, mesh=fine, in_specs=in_specs, out_specs=P(DP, HP), check_vma=False)

time: 185 us -> 174 us (0.941)
  Pallas kernels: 0 us -> 19.2 us
  waiting for transfers between devices: 59.4 us -> 42.1 us
  matrix products: 36.1 us -> 20.9 us
  other arithmetic: 8.54 us -> 1.27 us
  blocking collectives: 42.2 us -> 48.7 us
  local copies, waits for them, and re-layouts: 6.61 us -> 9.57 us
    all_to_all x0 -> x1, blocking collectives: none -> 31.7 us  [exchange(): return lax.all_to_all(x, axes, 0, 0, tiled=True)]
    all_to_all x2 -> x1, blocking collectives: 42.2 us -> 17 us  [from_everyone(): lax.all_to_all(jnp.broadcast_to(x[None], (devices, *x.shape)), axes, 0, 0...]
    all_to_all x4 -> x2, waiting for transfers between devices: 43.2 us -> 18.1 us  [exchange(): return lax.all_to_all(x, axes, 0, 0, tiled=True)]
    pallas_call x0 -> x3, Pallas kernels: none -> 19.2 us  [the longest x1 7.61 us: expand(): pl.pallas_call(kernel, in_specs=[VMEM] * 3 + [HBM] * len(weights), out_sp...]
    dot_general x7 -> x1, matrix products: 13.2 us -> 0.88 us  [dot(): return lax.dot_general(a, b, (dims, ((), ())), preferred_element_type=F32)]
    all_to_all x2 -> x3, starting transfers between devices: 7.61 us -> 18.4 us  [from_everyone(): lax.all_to_all(jnp.broadcast_to(x[None], (devices, *x.shape)), axes, 0, 0...]
    all_to_all x4 -> x2, starting transfers between devices: 22.3 us -> 11.6 us  [exchange(): return lax.all_to_all(x, axes, 0, 0, tiled=True)]
    all_to_all x2 -> x3, waiting for transfers between devices: 16.2 us -> 24 us  [from_everyone(): lax.all_to_all(jnp.broadcast_to(x[None], (devices, *x.shape)), axes, 0, 0...]
  transfers between devices with their start and end apart: 10 -> 9, of which waited for: 5 -> 4; matrix products, arithmetic and copies ran while one was open for 24% -> 16% of each run, Pallas kernels for 0% -> 0%
where the time goes in v2:
time: 174 us; the launch traced here: 173 us
  blocking collectives  48.7 us (28%)
  waiting for transfers between devices  42.1 us (24%)
  starting transfers between devices  30.6 us (18%)
  matrix products  20.9 us (12%)
  Pallas kernels  19.2 us (11%)
  local copies, waits for them, and re-layouts  9.57 us (6%)
    all_to_all x1, blocking collectives, exchange(): return lax.all_to_all(x, axes, 0, 0, tiled=True)  31.7 us
    all_to_all x3, waiting for transfers between devices, from_everyone(): lax.all_to_all(jnp.broadcast_to(x[None], (devices, *x.shape)), axes, 0, 0...  24 us
    all_to_all x3, starting transfers between devices, from_everyone(): lax.all_to_all(jnp.broadcast_to(x[None], (devices, *x.shape)), axes, 0, 0...  18.4 us
    all_to_all x2, waiting for transfers between devices, exchange(): return lax.all_to_all(x, axes, 0, 0, tiled=True)  18.1 us
    all_to_all x1, blocking collectives, from_everyone(): lax.all_to_all(jnp.broadcast_to(x[None], (devices, *x.shape)), axes, 0, 0...  17 us
    all_to_all x2, starting transfers between devices, exchange(): return lax.all_to_all(x, axes, 0, 0, tiled=True)  11.6 us
    dot_general x1, matrix products, attention(): jnp.einsum('shl,slc->shc', probs_bf, latent_cache[:, :, :latent_width], p...  9.03 us
    dot_general x1, matrix products, attention(): jnp.einsum('shc,slc->shl', query_full, latent_cache, preferred_element_ty...  7.92 us
  transfers between devices with their start and end apart: 9, of which 4 were waited for; matrix products, arithmetic and copies ran while one was open for 16% of the time, Pallas kernels for 0%

profile of v2, /device:TPU:0, one launch (start us, length us, event | category | flops | bytes accessed | tf_op | source)
XLA Modules:
  0.0 172.7 jit_solution(2379014420449957944)
XLA Ops:
  0.0 0.0 copy-start
  0.0 0.0 slice-start
  0.0 0.0 copy-start.7
  0.0 0.0 collective-permute-start
  0.0 1.8 %broadcast_in_dim.28 = bf16[8,32,896]{2,1,0:T(8,128)(2,1)} broadcast(bf16[32,896]{1,0:T(8,128)(2,1)} %param.12), dimensions={1,2} | broadcast | bytes 516096 | tf_op jit(solution)/shard_map/broadcast_in_dim | solution.py:22
  1.8 7.1 %all-to-all-start = ((bf16[8,32,896]{2,1,0:T(8,128)(2,1)}), bf16[8,32,896]{2,1,0:T(8,128)(2,1)}, u32[]{:S(2)}, u32[]{:S(2)}) async-start(bf16[8,32,896]{2,1,0:T(8,128)(2,1)} %broadcast_in_dim.28), calls=%async_computation | async-start | bytes 917504 | tf_op jit(solution)/shard_map/all_to_all | solution.py:22
  9.0 0.1 collective-permute-start.1
  9.0 0.4 collective-permute-start.2
  9.5 0.1 collective-permute-start.3
  9.6 0.9 slice.22
  10.5 0.0 copy-done.7
  10.5 0.0 copy-start.5
  10.5 0.1 iota_compare_fusion.1
  10.6 0.0 copy-done
  10.6 0.0 slice-done
  10.6 0.4 fusion.9
  11.0 0.1 pad_maximum_fusion
  11.1 0.2 copy-done.5
  11.3 0.4 fusion.14
  11.7 7.9 %fusion.29 = (f32[32,16]{1,0:T(8,128)S(1)}, f32[32,16,512]{2,1,0:T(8,128)S(1)}) fusion(bf16[32,512,576]{1,2,0:T(8,128)(2,1)} %param.14, bf16[32,16,576]{2,0,1:T(8,128)(2,1)S(1)} %pad_maximum_fusion, pred[32,512]{1,0:T(8,128)(4,1)S(1)} %iota_compare_fusion.1), kind=kOutput, calls=%fused_computation.46 | convolution fusion | flops 302775808 | bytes 20531200 | tf_op jit(solution)/shard_map/shc,slc->shl/dot_general | solution.py:141
  19.6 0.3 fusion.13
  20.0 9.0 %fusion.6 = bf16[32,16,512]{2,1,0:T(8,128)(2,1)} fusion(bf16[32,512,576]{1,2,0:T(8,128)(2,1)} %param.14, f32[32,16,512]{2,1,0:T(8,128)S(1)} %get-tuple-element.24, f32[32,512]{1,0:T(8,128)S(1)} %slice_convert_fusion, f32[32,16]{1,0:T(8,128)S(1)} %get-tuple-element.22, f32[32,16]{1,0:T(8,128)S(1)} %get-tuple-element.21, f32[32,16]{1,0:T(8,128)S(1)} %multiply_maximum_fusion), kind=kOutput, calls=%fused_computation.6 | convolution fusion | flops 270008320 | bytes 18421760 | tf_op jit(solution)/shard_map/shl,slc->shc/dot_general | solution.py:156
  29.0 0.0 all-to-all-done
  29.0 0.0 collective-permute-done
  29.0 2.4 %fusion.10 = bf16[16,4,8,128]{3,2,1,0:T(8,128)(2,1)S(1)} fusion(bf16[16,512,128]{2,1,0:T(8,128)(2,1)} %param.18, bf16[32,16,512]{2,1,0:T(8,128)(2,1)} %fusion.6), kind=kOutput, calls=%fused_computation.10 | convolution fusion | flops 67174400 | bytes 2752512 | tf_op jit(solution)/shard_map/shc,hcv->shv/dot_general | solution.py:193
  31.4 1.2 broadcast_in_dim.52
  32.6 7.1 %all-to-all-start.1 = ((bf16[8,32,2048]{2,1,0:T(8,128)(2,1)}), bf16[8,32,2048]{2,1,0:T(8,128)(2,1)S(1)}, u32[]{:S(2)}, u32[]{:S(2)}) async-start(bf16[8,32,2048]{2,1,0:T(8,128)(2,1)} %broadcast_in_dim.52), calls=%async_computation.1 | async-start | bytes 2097152 | tf_op jit(solution)/shard_map/all_to_all | solution.py:22
  39.7 2.0 %copy.25 = bf16[256,896]{0,1:T(8,128)(2,1)} copy(bf16[256,896]{1,0:T(8,128)(2,1)} %bitcast.4) | data formatting | bytes 917504 | tf_op jit(solution)/shard_map/optimization_barrier | solution.py:190
  41.7 0.0 collective-permute-done.1.refs_1_
  41.7 0.0 collective-permute-done.2.refs_3_
  41.7 0.0 collective-permute-done.3.refs_1_
  41.7 15.3 %all-to-all-done.1 = bf16[8,32,2048]{2,1,0:T(8,128)(2,1)S(1)} async-done(((bf16[8,32,2048]{2,1,0:T(8,128)(2,1)}), bf16[8,32,2048]{2,1,0:T(8,128)(2,1)S(1)}, u32[]{:S(2)}, u32[]{:S(2)}) %all-to-all-start.1) | async-done | bytes 1048608 | tf_op jit(solution)/shard_map/all_to_all | solution.py:22
  57.0 0.0 copy-start.1
  57.0 1.1 copy-done.1
  58.1 5.8 %project.1 = bf16[8,2,56,256]{3,2,1,0:T(8,128)(2,1)} custom-call(bf16[256,2048]{1,0:T(8,128)(2,1)} %bitcast.30, bf16[448,2048]{1,0:T(8,128)(2,1)} %bitcast.34, bf16[448,2048]{1,0:T(8,128)(2,1)} %bitcast.11.refs_1_), custom_call_target="tpu_custom_call" | custom-call | tf_op jit(solution)/shard_map/project/pallas_call | solution.py:70
  63.9 0.0 copy-start.6
  63.9 5.4 %all-to-all-start.2 = ((bf16[8,2,56,256]{3,2,1,0:T(8,128)(2,1)}), bf16[8,2,56,256]{3,2,1,0:T(8,128)(2,1)S(1)}, u32[]{:S(2)}, u32[]{:S(2)}) async-start(bf16[8,2,56,256]{3,2,1,0:T(8,128)(2,1)} %project.1), calls=%async_computation.2 | async-start | bytes 917504 | tf_op jit(solution)/shard_map/all_to_all | solution.py:26
  69.3 8.9 %all-to-all-done.2 = bf16[8,2,56,256]{3,2,1,0:T(8,128)(2,1)S(1)} async-done(((bf16[8,2,56,256]{3,2,1,0:T(8,128)(2,1)}), bf16[8,2,56,256]{3,2,1,0:T(8,128)(2,1)S(1)}, u32[]{:S(2)}, u32[]{:S(2)}) %all-to-all-start.2) | async-done | bytes 458784 | tf_op jit(solution)/shard_map/all_to_all | solution.py:26
  78.3 0.1 reduce_sum.49
  78.3 0.8 broadcast_in_dim.53
  79.2 4.2 %all-to-all-start.3 = ((bf16[8,2,56,256]{3,2,1,0:T(8,128)(2,1)}), bf16[8,2,56,256]{3,2,1,0:T(8,128)(2,1)S(1)}, u32[]{:S(2)}, u32[]{:S(2)}) async-start(bf16[8,2,56,256]{3,2,1,0:T(8,128)(2,1)} %broadcast_in_dim.53), calls=%async_computation.3 | async-start | bytes 917504 | tf_op jit(solution)/shard_map/all_to_all | solution.py:22
  83.4 0.0 copy-done.6
  83.4 0.6 reshape.70.gain
  83.9 8.7 %all-to-all-done.3 = bf16[8,2,56,256]{3,2,1,0:T(8,128)(2,1)S(1)} async-done(((bf16[8,2,56,256]{3,2,1,0:T(8,128)(2,1)}), bf16[8,2,56,256]{3,2,1,0:T(8,128)(2,1)S(1)}, u32[]{:S(2)}, u32[]{:S(2)}) %all-to-all-start.3) | async-done | bytes 458784 | tf_op jit(solution)/shard_map/all_to_all | solution.py:22
  92.6 0.0 copy-start.2
  92.6 0.8 copy-done.2
  93.4 7.6 %expand.1 = bf16[256,4736]{1,0:T(8,128)(2,1)} custom-call(bf16[896,256]{1,0:T(8,128)(2,1)} %bitcast.35, bf16[896,256]{1,0:T(8,128)(2,1)} %bitcast.31, f32[1,896]{1,0:T(1,128)} %reshape.70.gain, bf16[896,1152]{1,0:T(8,128)(2,1)} %refs_0_.2, bf16[896,1152]{1,0:T(8,128)(2,1)} %collective-permute-done.1.refs_1_, bf16[896,1152]{1,0:T(8,128)(2,1)} %refs_2_.1, ...), custom_call_target="tpu_custom_call" | custom-call | tf_op jit(solution)/shard_map/expand/pallas_call | solution.py:100
  101.0 31.7 %all_to_all.35 = bf16[8,32,4736]{2,1,0:T(8,128)(2,1)S(1)} all-to-all(bf16[8,32,4736]{2,1,0:T(8,128)(2,1)} %bitcast.28), channel_id=1, replica_groups=mesh['x'=4,'h'=2,'c'=2,'z'=4,'l'=2] {'z','l'}, dimensions={0} | all-to-all | bytes 4849664 | tf_op jit(solution)/shard_map/all_to_all | solution.py:26
  132.8 0.3 convert_reduce_fusion
  133.1 0.1 slice_reduce_fusion
  133.2 0.2 fusion.21
  133.4 0.1 broadcast_in_dim.56
  133.5 17.0 %all_to_all.36 = bf16[8,32,2304]{2,1,0:T(8,128)(2,1)} all-to-all(bf16[8,32,2304]{2,1,0:T(8,128)(2,1)S(1)} %broadcast_in_dim.56), channel_id=1, replica_groups=mesh['x'=4,'h'=2,'c'=2,'z'=4,'l'=2] {'z','l'}, dimensions={0} | all-to-all | bytes 2359296 | tf_op jit(solution)/shard_map/all_to_all | solution.py:22
  150.5 0.0 copy-start.3
  150.5 0.0 copy-start.4
  150.5 5.8 %contract.1 = bf16[256,896]{1,0:T(8,128)(2,1)} custom-call(bf16[256,2304]{1,0:T(8,128)(2,1)} %bitcast.29, bf16[1152,896]{1,0:T(8,128)(2,1)} %refs_0_.3, bf16[1152,896]{1,0:T(8,128)(2,1)} %collective-permute-done.3.refs_1_), custom_call_target="tpu_custom_call" | custom-call | tf_op jit(solution)/shard_map/contract/pallas_call | solution.py:122
  156.3 6.1 %all-to-all-start.6 = ((bf16[8,32,896]{2,1,0:T(8,128)(2,1)}), bf16[8,32,896]{2,1,0:T(8,128)(2,1)S(1)}, u32[]{:S(2)}, u32[]{:S(2)}) async-start(bf16[8,32,896]{2,1,0:T(8,128)(2,1)} %bitcast.33), calls=%async_computation.6 | async-start | bytes 917504 | tf_op jit(solution)/shard_map/all_to_all | solution.py:26
  162.4 9.2 %all-to-all-done.6 = bf16[8,32,896]{2,1,0:T(8,128)(2,1)S(1)} async-done(((bf16[8,32,896]{2,1,0:T(8,128)(2,1)}), bf16[8,32,896]{2,1,0:T(8,128)(2,1)S(1)}, u32[]{:S(2)}, u32[]{:S(2)}) %all-to-all-start.6) | async-done | bytes 458784 | tf_op jit(solution)/shard_map/all_to_all | solution.py:26
  171.7 0.1 convert_reduce_fusion.1
  171.8 0.0 copy-done.3
  171.8 0.0 copy-done.4
  171.8 0.9 fusion.12
  (8 shorter events, 0.1 us)
Async XLA Ops:
  0.0 10.6 %copy-start = (bf16[16,128,512]{2,1,0:T(8,128)(2,1)S(1)}, bf16[16,128,512]{2,1,0:T(8,128)(2,1)}, u32[]{:S(2)}) copy-start(bf16[16,128,512]{2,1,0:T(8,128)(2,1)} %param.17) | copy-start | bytes 6291460
  0.0 10.6 %slice-start = ((bf16[32,16,192]{2,1,0:T(8,128)(2,1)}), bf16[32,16,128]{2,1,0:T(8,128)(2,1)S(1)}, s32[]{:S(2)}) async-start(bf16[32,16,192]{2,1,0:T(8,128)(2,1)} %param.13), calls=%async_computation.7 | async-start | bytes 262144 | tf_op jit(solution)/shard_map/slice | solution.py:137
  0.0 10.5 %copy-start.7 = (s32[32]{0:T(128)S(1)}, s32[32]{0:T(128)}, u32[]{:S(2)}) copy-start(s32[32]{0:T(128)} %param.16) | copy-start | bytes 388
  0.0 29.0 %collective-permute-start = (bf16[2048,8,56]{0,2,1:T(8,128)(2,1)}, bf16[2048,8,56]{0,2,1:T(8,128)(2,1)}, u32[]{:S(2)}, u32[]{:S(2)}) collective-permute-start(bf16[2048,8,56]{0,2,1:T(8,128)(2,1)} %param.19), channel_id=1, source_target_pairs={{0,8},{8,0},{1,9},{9,1},{2,10},{10,2},{3,11},{11,3},{4,12},{12,4},... | collective-permute-start | bytes 5505032 | tf_op jit(solution)/shard_map/ppermute | solution.py:34
  1.8 27.2 %all-to-all-start = ((bf16[8,32,896]{2,1,0:T(8,128)(2,1)}), bf16[8,32,896]{2,1,0:T(8,128)(2,1)}, u32[]{:S(2)}, u32[]{:S(2)}) async-start(bf16[8,32,896]{2,1,0:T(8,128)(2,1)} %broadcast_in_dim.28), calls=%async_computation | async-start | bytes 917504 | tf_op jit(solution)/shard_map/all_to_all | solution.py:22
  9.0 32.8 %collective-permute-start.1 = (bf16[896,1152]{1,0:T(8,128)(2,1)}, bf16[896,1152]{1,0:T(8,128)(2,1)}, u32[]{:S(2)}, u32[]{:S(2)}) collective-permute-start(bf16[896,1152]{1,0:T(8,128)(2,1)} %refs_0_.2), channel_id=1, source_target_pairs={{0,8},{8,0},{1,9},{9,1},{2,10},{10,2},{3,11},{11,3},{4,12},{12,4},... | collective-permute-start | bytes 6193160 | tf_op jit(solution)/shard_map/ppermute | solution.py:34
  9.0 32.7 %collective-permute-start.2 = (bf16[896,1152]{1,0:T(8,128)(2,1)}, bf16[896,1152]{1,0:T(8,128)(2,1)}, u32[]{:S(2)}, u32[]{:S(2)}) collective-permute-start(bf16[896,1152]{1,0:T(8,128)(2,1)} %refs_2_.1), channel_id=1, source_target_pairs={{0,8},{8,0},{1,9},{9,1},{2,10},{10,2},{3,11},{11,3},{4,12},{12,4},... | collective-permute-start | bytes 6193160 | tf_op jit(solution)/shard_map/ppermute | solution.py:34
  9.5 32.3 %collective-permute-start.3 = (bf16[1152,896]{1,0:T(8,128)(2,1)}, bf16[1152,896]{1,0:T(8,128)(2,1)}, u32[]{:S(2)}, u32[]{:S(2)}) collective-permute-start(bf16[1152,896]{1,0:T(8,128)(2,1)} %refs_0_.3), channel_id=1, source_target_pairs={{0,8},{8,0},{1,9},{9,1},{2,10},{10,2},{3,11},{11,3},{4,12},{12,4},... | collective-permute-start | bytes 6193160 | tf_op jit(solution)/shard_map/ppermute | solution.py:34
  10.5 0.8 copy-start.5
  32.6 24.5 %all-to-all-start.1 = ((bf16[8,32,2048]{2,1,0:T(8,128)(2,1)}), bf16[8,32,2048]{2,1,0:T(8,128)(2,1)S(1)}, u32[]{:S(2)}, u32[]{:S(2)}) async-start(bf16[8,32,2048]{2,1,0:T(8,128)(2,1)} %broadcast_in_dim.52), calls=%async_computation.1 | async-start | bytes 2097152 | tf_op jit(solution)/shard_map/all_to_all | solution.py:22
  57.0 1.1 copy-start.1
  63.9 19.5 %copy-start.6 = (bf16[896]{0:T(1024)(128)(2,1)S(1)}, bf16[896]{0:T(1024)(128)(2,1)}, u32[]{:S(2)}) copy-start(bf16[896]{0:T(1024)(128)(2,1)} %param.20) | copy-start | bytes 5380
  63.9 14.3 %all-to-all-start.2 = ((bf16[8,2,56,256]{3,2,1,0:T(8,128)(2,1)}), bf16[8,2,56,256]{3,2,1,0:T(8,128)(2,1)S(1)}, u32[]{:S(2)}, u32[]{:S(2)}) async-start(bf16[8,2,56,256]{3,2,1,0:T(8,128)(2,1)} %project.1), calls=%async_computation.2 | async-start | bytes 917504 | tf_op jit(solution)/shard_map/all_to_all | solution.py:26
  79.2 13.4 %all-to-all-start.3 = ((bf16[8,2,56,256]{3,2,1,0:T(8,128)(2,1)}), bf16[8,2,56,256]{3,2,1,0:T(8,128)(2,1)S(1)}, u32[]{:S(2)}, u32[]{:S(2)}) async-start(bf16[8,2,56,256]{3,2,1,0:T(8,128)(2,1)} %broadcast_in_dim.53), calls=%async_computation.3 | async-start | bytes 917504 | tf_op jit(solution)/shard_map/all_to_all | solution.py:22
  92.6 0.8 copy-start.2
  150.5 21.3 %copy-start.3 = (bf16[8,2,56,256]{3,2,1,0:T(8,128)(2,1)S(1)}, bf16[8,2,56,256]{3,2,1,0:T(8,128)(2,1)}, u32[]{:S(2)}) copy-start(bf16[8,2,56,256]{3,2,1,0:T(8,128)(2,1)} %copy-done.2) | copy-start | bytes 1376260
  150.5 21.3 %copy-start.4 = (bf16[32,896]{1,0:T(8,128)(2,1)S(1)}, bf16[32,896]{1,0:T(8,128)(2,1)}, u32[]{:S(2)}) copy-start(bf16[32,896]{1,0:T(8,128)(2,1)} %param.12) | copy-start | bytes 172036
  156.3 15.4 %all-to-all-start.6 = ((bf16[8,32,896]{2,1,0:T(8,128)(2,1)}), bf16[8,32,896]{2,1,0:T(8,128)(2,1)S(1)}, u32[]{:S(2)}, u32[]{:S(2)}) async-start(bf16[8,32,896]{2,1,0:T(8,128)(2,1)} %bitcast.33), calls=%async_computation.6 | async-start | bytes 917504 | tf_op jit(solution)/shard_map/all_to_all | solution.py:26

commit v3 on v1

v3 whole, which is shorter than its diff:
```python
import functools
import math

import jax
import jax.numpy as jnp
from jax import lax
from jax.experimental import pallas as pl
from jax.experimental.pallas import tpu as pltpu
from jax.sharding import Mesh, PartitionSpec as P


D = 7168
LANES = 128
GROUP = 8
F32 = jnp.float32
BF16 = jnp.bfloat16
DP = ("x", "h", "c")
CHIPS = ("x", "h")
HP = ("z", "l")


def from_everyone(x, axes):
    devices = lax.axis_size(axes)
    return lax.all_to_all(jnp.broadcast_to(x[None], (devices, *x.shape)), axes, 0, 0, tiled=True)


def exchange(x, axes):
    return lax.all_to_all(x, axes, 0, 0, tiled=True)


def dot(a, b, dims):
    return lax.dot_general(a, b, (dims, ((), ())), preferred_element_type=F32)


def other_core(w):
    return lax.ppermute(w, "c", [(0, 1), (1, 0)])


VMEM = pl.BlockSpec(memory_space=pltpu.VMEM)
HBM = pl.BlockSpec(memory_space=pl.ANY)


def expand(places, residuals, attention_cols, gain, weights):
    width, tokens = attention_cols.shape
    units = weights[0].shape[1]
    steps, sides, rows = len(residuals), *residuals[0].shape[:2]

    def kernel(places, attention_out, gain, *refs):
        pieces, sources = refs[:steps], refs[steps : steps + len(weights)]
        out, ready, slots, sums, power_slot, sems = refs[steps + len(weights) :]

        def copy(i, source, target):
            return pltpu.make_async_copy(source, target, sems.at[i])

        first = [copy(i, piece, ready.at[i]) for i, piece in enumerate(pieces)]
        second = [copy(steps + i, w, slots.at[i]) for i, w in enumerate(sources)]
        for c in first + second:
            c.start()
        across = attention_out[...].T.astype(F32)
        for c in first:
            c.wait()
        blocks = []
        for x in range(steps):
            for h in range(sides):
                there = ready[
                    lax.rem(x - places[0] + steps, steps), lax.rem(h - places[1] + sides, sides)
                ]
                at = (x * sides + h) * rows
                blocks.append(there.astype(F32) + across[at : at + rows])
        hidden = jnp.concatenate(blocks, axis=0)
        power = jnp.sum(hidden * hidden, axis=1, keepdims=True)
        high = power.astype(BF16).astype(F32)
        middle = (power - high).astype(BF16).astype(F32)
        low = power - high - middle
        lane = lax.broadcasted_iota(jnp.int32, (tokens, LANES), 1)
        parts = jnp.where(lane == 0, high, jnp.where(lane == 1, middle, low))
        power_slot[...] = jnp.where(lane < 3, parts, 0.0).astype(BF16)
        base = steps + len(weights)
        last = [copy(base, power_slot, out.at[:, len(weights) * units :])]
        last[0].start()
        scaled = (hidden * gain[...]).astype(BF16)
        for i, c in enumerate(second):
            c.wait()
            sums[i] = dot(scaled, slots[i], ((1,), (0,))).astype(BF16)
            last.append(copy(base + 1 + i, sums.at[i], out.at[:, i * units : (i + 1) * units]))
            last[-1].start()
        for c in last:
            c.wait()

    return pl.pallas_call(
        kernel,
        in_specs=[pl.BlockSpec(memory_space=pltpu.SMEM), VMEM, VMEM]
        + [HBM] * (steps + len(weights)),
        out_specs=HBM,
        out_shape=jax.ShapeDtypeStruct((tokens, len(weights) * units + LANES), BF16),
        scratch_shapes=[
            pltpu.VMEM((steps, sides, rows, width), BF16),
            pltpu.VMEM((len(weights), width, units), BF16),
            pltpu.VMEM((len(weights), tokens, units), BF16),
            pltpu.VMEM((tokens, LANES), BF16),
            pltpu.SemaphoreType.DMA((steps + 2 * len(weights) + 1,)),
        ],
        name="expand",
    )(places, attention_cols, gain, *residuals, *weights)


def attend(lengths, query_full, new_latent, cache_cols, latent_width, softmax_scale):
    samples, heads, entry = query_full.shape
    slots = cache_cols.shape[2]
    blocks = slots // LANES
    groups = samples // GROUP

    def kernel(lengths, query, new, cache, out, buf, fresh, order, sems):
        def live(s):
            return lax.div(lengths[s] + (LANES - 1), LANES)

        def tally(s, counts):
            return tuple(c + (live(s) == k + 1).astype(jnp.int32) for k, c in enumerate(counts))

        counts = lax.fori_loop(0, samples, tally, (jnp.int32(0),) * blocks)
        ends = [jnp.int32(0)]
        for c in counts[:-1]:
            ends.append(ends[-1] + c)

        def place(s, ends):
            at = ends[0]
            for k in range(1, blocks):
                at = jnp.where(live(s) == k + 1, ends[k], at)
            order[at] = s
            return tally(s, ends)

        lax.fori_loop(0, samples, place, tuple(ends))

        def by_size(i, act):
            last = live(order[i * GROUP + GROUP - 1])
            for k in range(1, blocks + 1):
                pl.when(last == k)(functools.partial(act, i, k * LANES))

        def copies(act, i, size):
            for g in range(GROUP):
                slot = lax.rem(i, 2) * GROUP + g
                act(
                    pltpu.make_async_copy(
                        cache.at[order[i * GROUP + g], :, :size],
                        buf.at[slot, :, :size],
                        sems.at[slot],
                    )
                )

        start = functools.partial(copies, lambda copy: copy.start())
        wait = functools.partial(copies, lambda copy: copy.wait())
        by_size(0, start)
        by_size(1, start)
        for s in range(samples):
            fresh[s] = new[s : s + 1, :].astype(F32)

        def mix(i, size):
            half = lax.rem(i, 2) * GROUP
            scores, own = [], []
            for g in range(GROUP):
                s = order[i * GROUP + g]
                q = query[s]
                part = dot(q, buf[half + g, :, :size], ((1,), (0,))) * softmax_scale
                positions = lax.broadcasted_iota(jnp.int32, part.shape, 1)
                scores.append(jnp.where(positions < lengths[s], part, -1e30))
                own.append(jnp.sum(q.astype(F32) * fresh[s], axis=1, keepdims=True))
            scores = jnp.concatenate(scores, axis=0)
            own = jnp.concatenate(own, axis=0) * softmax_scale
            peak = jnp.maximum(jnp.max(scores, axis=1, keepdims=True), own)
            cached_exp = jnp.exp(scores - peak)
            own_exp = jnp.exp(own - peak)
            total = jnp.sum(cached_exp, axis=1, keepdims=True) + own_exp
            probs = (cached_exp / total).astype(BF16)
            own_prob = (own_exp / total).astype(BF16).astype(F32)
            for g in range(GROUP):
                s = order[i * GROUP + g]
                mine = slice(g * heads, (g + 1) * heads)
                values = buf[half + g, :latent_width, :size]
                mixed = dot(values, probs[mine], ((1,), (1,))).T
                out[s] = (mixed + own_prob[mine] * fresh[s][:, :latent_width]).astype(BF16)

        def step(i, carry):
            by_size(i, wait)
            by_size(i, mix)

            @pl.when(i + 2 < groups)
            def _():
                by_size(i + 2, start)

            return carry

        lax.fori_loop(0, groups, step, 0)

    return pl.pallas_call(
        kernel,
        in_specs=[pl.BlockSpec(memory_space=pltpu.SMEM), VMEM, VMEM, HBM],
        out_specs=VMEM,
        out_shape=jax.ShapeDtypeStruct((samples, heads, latent_width), BF16),
        scratch_shapes=[
            pltpu.VMEM((2 * GROUP, entry, slots), BF16),
            pltpu.VMEM((samples, 1, entry), F32),
            pltpu.SMEM((samples,), jnp.int32),
            pltpu.SemaphoreType.DMA((2 * GROUP,)),
        ],
        name="attend",
    )(lengths, query_full, new_latent, cache_cols)


def attention(queries, latent_cache, new_latent, lengths, w_absorb):
    nope_width = w_absorb.shape[1]
    query_latent = jnp.einsum(
        "shn,hnc->shc", queries[:, :, :nope_width], w_absorb, preferred_element_type=F32
    ).astype(BF16)
    query_full = jnp.concatenate([query_latent, queries[:, :, nope_width:]], axis=2)
    return attend(
        lengths,
        query_full,
        new_latent,
        latent_cache.swapaxes(1, 2),
        w_absorb.shape[2],
        1.0 / math.sqrt(queries.shape[2]),
    )


def layer(
    residual,
    queries,
    latent_cache,
    new_latent,
    lengths,
    w_absorb,
    w_value,
    w_out,
    norm_gain,
    w_gate,
    w_up,
    w_down,
):
    rows = queries.shape[0]
    width = residual.shape[1]
    core = lax.axis_index("c")
    chip = lax.axis_index(CHIPS)
    w_out_other = other_core(w_out)
    w_gate_other = other_core(w_gate)
    w_up_other = other_core(w_up)
    w_down_other = other_core(w_down)

    head_latent = attention(queries, latent_cache, new_latent, lengths, w_absorb)
    head_latent, w_out_other = lax.optimization_barrier((head_latent, w_out_other))
    head_values = jnp.einsum("shc,hcv->shv", head_latent, w_value, preferred_element_type=F32)
    head_values = head_values.astype(BF16).reshape(rows, -1)
    all_values = from_everyone(head_values, CHIPS).reshape(-1, head_values.shape[1])
    across = lax.ppermute(residual, "h", [(0, 1), (1, 0)])
    all_values, across, w_gate_other, w_up_other, w_down_other = lax.optimization_barrier(
        (all_values, across, w_gate_other, w_up_other, w_down_other)
    )
    tokens = all_values.shape[0]

    partial = jnp.stack(
        [
            jnp.einsum("tk,kbf->bft", all_values, w, preferred_element_type=F32).astype(BF16)
            for w in (w_out, w_out_other)
        ],
        axis=1,
    )
    arrived = exchange(partial, HP)
    both_rows = jnp.stack([residual, across])
    steps = lax.axis_size("x")
    residuals = [both_rows] + [
        lax.ppermute(both_rows, "x", [((i + step) % steps, i) for i in range(steps)])
        for step in range(1, steps)
    ]
    arrived, *residuals = lax.optimization_barrier((arrived, *residuals))
    summed = arrived.astype(F32).sum(axis=0).astype(BF16)
    summed = jnp.where(core == 0, summed, summed[::-1])
    attention_cols = from_everyone(summed, CHIPS).reshape(width, tokens)

    both = expand(
        jnp.stack([lax.axis_index("x"), lax.axis_index("h")]),
        residuals,
        attention_cols,
        norm_gain.astype(F32)[None, :],
        (w_gate, w_gate_other, w_up, w_up_other),
    )
    both = exchange(both.reshape(lax.axis_size(HP), -1, both.shape[1]), HP)
    both = both.astype(F32).sum(axis=0)
    units = both.shape[1] // 2 - LANES // 2
    row_power = jnp.sum(both[:, 2 * units :], axis=1, keepdims=True) / D
    factor = lax.rsqrt(row_power + 1e-06)
    gate_sum = both[:, :units] * factor
    up_sum = both[:, units : 2 * units] * factor
    share = (jax.nn.silu(gate_sum) * up_sum).astype(BF16)
    activated = from_everyone(share, HP).reshape(tokens, -1)

    own_units = w_down.shape[0]
    ffn = sum(
        dot(activated[:, i * own_units : (i + 1) * own_units], w, ((1,), (0,)))
        for i, w in enumerate((w_down, w_down_other))
    ).astype(BF16)
    ffn = exchange(ffn.reshape(-1, rows, width), CHIPS).astype(F32).sum(axis=0)

    pick = (
        lax.broadcasted_iota(jnp.int32, (tokens, rows), 0)
        == lax.broadcasted_iota(jnp.int32, (tokens, rows), 1) + chip * rows
    ).astype(BF16)
    own_attention = dot(pick, attention_cols, ((0,), (1,)))
    own_hidden = residual.astype(F32) + own_attention
    return (own_hidden + ffn).astype(BF16)


def solution(mesh):
    fine = Mesh(mesh.devices.reshape(4, 2, 2, 4, 2), ("x", "h", "c", "z", "l"))
    in_specs = (
        P(DP, HP),
        P(DP, HP, None),
        P(DP, None, None),
        P(DP, None),
        P(DP),
        P(HP, None, None),
        P(HP, None, None),
        P(HP, None, DP),
        P(HP),
        P(HP, DP),
        P(HP, DP),
        P(DP, HP),
    )
    return jax.shard_map(layer, mesh=fine, in_specs=in_specs, out_specs=P(DP, HP), check_vma=False)
```

time: 185 us -> 159 us (0.86)
  matrix products: 36.1 us -> 10.7 us
  waiting for transfers between devices: 59.4 us -> 34.1 us
  Pallas kernels: 0 us -> 19.1 us
  blocking collectives: 42.2 us -> 49.6 us
  starting transfers between devices: 30.4 us -> 36.8 us
  other arithmetic: 8.54 us -> 2.39 us
    all_to_all x4 -> x2, waiting for transfers between devices: 43.2 us -> 9.24 us  [exchange(): return lax.all_to_all(x, axes, 0, 0, tiled=True)]
    all_to_all x0 -> x1, blocking collectives: none -> 32.9 us  [exchange(): return lax.all_to_all(x, axes, 0, 0, tiled=True)]
    all_to_all x2 -> x1, blocking collectives: 42.2 us -> 16.7 us  [from_everyone(): lax.all_to_all(jnp.broadcast_to(x[None], (devices, *x.shape)), axes, 0, 0...]
    pallas_call x0 -> x2, Pallas kernels: none -> 19.1 us  [the longest x1 11.9 us: attend(): pl.pallas_call(kernel, in_specs=[pl.BlockSpec(memory_space=pltpu.SMEM), V...]
    ppermute x0 -> x4, waiting for transfers between devices: none -> 16.4 us  [the longest x1 13.1 us: layer(): across = lax.ppermute(residual, 'h', [(0, 1), (1, 0)])]
    dot_general x4 -> x2, matrix products: 19.7 us -> 4.67 us  [the longest x1 2.36 us: layer(): jnp.einsum('shc,hcv->shv', head_latent, w_value, preferred_element_type=F32)]
    ppermute x0 -> x4, starting transfers between devices: none -> 9.19 us  [the longest x3 5.67 us: layer(): lax.ppermute(both_rows, 'x', [((i + step) % steps, i) for i in range(step...]
    all_to_all x4 -> x2, starting transfers between devices: 22.3 us -> 13.9 us  [exchange(): return lax.all_to_all(x, axes, 0, 0, tiled=True)]
  transfers between devices with their start and end apart: 10 -> 12, of which waited for: 5 -> 6; matrix products, arithmetic and copies ran while one was open for 24% -> 5% of each run, Pallas kernels for 0% -> 8%
where the time goes in v3:
time: 159 us; the launch traced here: 158 us
  blocking collectives  49.6 us (31%)
  starting transfers between devices  36.8 us (23%)
  waiting for transfers between devices  34.1 us (21%)
  Pallas kernels  19.1 us (12%)
  matrix products  10.7 us (7%)
  local copies, waits for them, and re-layouts  5.59 us (4%)
  other arithmetic  2.39 us (2%)
    all_to_all x1, blocking collectives, exchange(): return lax.all_to_all(x, axes, 0, 0, tiled=True)  32.9 us
    all_to_all x1, blocking collectives, from_everyone(): lax.all_to_all(jnp.broadcast_to(x[None], (devices, *x.shape)), axes, 0, 0...  16.7 us
    all_to_all x2, starting transfers between devices, exchange(): return lax.all_to_all(x, axes, 0, 0, tiled=True)  13.9 us
    ppermute x1, waiting for transfers between devices, layer(): across = lax.ppermute(residual, 'h', [(0, 1), (1, 0)])  13.1 us
    all_to_all x2, starting transfers between devices, from_everyone(): lax.all_to_all(jnp.broadcast_to(x[None], (devices, *x.shape)), axes, 0, 0...  12.7 us
    pallas_call x1, Pallas kernels, attend(): pl.pallas_call(kernel, in_specs=[pl.BlockSpec(memory_space=pltpu.SMEM), V...  11.9 us
    all_to_all x2, waiting for transfers between devices, exchange(): return lax.all_to_all(x, axes, 0, 0, tiled=True)  9.24 us
    all_to_all x2, waiting for transfers between devices, from_everyone(): lax.all_to_all(jnp.broadcast_to(x[None], (devices, *x.shape)), axes, 0, 0...  8.45 us
  transfers between devices with their start and end apart: 12, of which 6 were waited for; matrix products, arithmetic and copies ran while one was open for 5% of the time, Pallas kernels for 8%

profile of v3, /device:TPU:0, one launch (start us, length us, event | category | flops | bytes accessed | tf_op | source)
XLA Modules:
  0.0 158.5 jit_solution(12605901303677063832)
XLA Ops:
  0.0 0.0 copy-start
  0.0 0.0 collective-permute-start
  0.0 0.5 collective-permute-start.2
  0.5 0.0 collective-permute-start.3
  0.5 0.5 collective-permute-start.4
  1.0 0.9 slice.21
  2.0 0.0 copy-done
  2.0 0.4 fusion.13
  2.4 0.3 copy.40
  2.7 0.0 slice-done
  2.7 0.9 pad_maximum_fusion.query
  3.6 11.9 %attend.1 = bf16[32,16,512]{2,1,0:T(8,128)(2,1)} custom-call(s32[32]{0:T(128)} %lengths.1, bf16[32,16,576]{2,1,0:T(8,128)(2,1)} %pad_maximum_fusion.query, bf16[32,576]{1,0:T(8,128)(2,1)} %new.1, bf16[32,576,512]{2,1,0:T(8,128)(2,1)} %bitcast.38), custom_call_target="tpu_custom_call" | custom-call | tf_op jit(solution)/shard_map/attend/pallas_call | solution.py:194
  15.5 0.0 collective-permute-done
  15.6 2.4 %fusion.2 = bf16[16,4,8,128]{3,2,1,0:T(8,128)(2,1)S(1)} fusion(bf16[16,512,128]{2,1,0:T(8,128)(2,1)} %param.18, bf16[32,16,512]{2,1,0:T(8,128)(2,1)} %attend.1), kind=kOutput, calls=%fused_computation.6 | convolution fusion | flops 67174400 | bytes 2752512 | tf_op jit(solution)/shard_map/shc,hcv->shv/dot_general | solution.py:250
  17.9 0.0 copy-start.6
  18.0 1.2 broadcast_in_dim.26
  19.1 7.3 %all-to-all-start = ((bf16[8,32,2048]{2,1,0:T(8,128)(2,1)}), bf16[8,32,2048]{2,1,0:T(8,128)(2,1)S(1)}, u32[]{:S(2)}, u32[]{:S(2)}) async-start(bf16[8,32,2048]{2,1,0:T(8,128)(2,1)} %broadcast_in_dim.26), calls=%async_computation | async-start | bytes 2097152 | tf_op jit(solution)/shard_map/all_to_all | solution.py:24
  26.5 0.0 copy-done.6
  26.5 3.5 %collective-permute-start.1 = (bf16[32,896]{1,0:T(8,128)(2,1)S(1)}, bf16[32,896]{1,0:T(8,128)(2,1)S(1)}, u32[]{:S(2)}, u32[]{:S(2)}) collective-permute-start(bf16[32,896]{1,0:T(8,128)(2,1)S(1)} %copy-done.6), channel_id=1, source_target_pairs={{0,16},{16,0},{1,17},{17,1},{2,18},{18,2},{3,19},{19,3},{4,20},{20... | collective-permute-start | bytes 172040 | tf_op jit(solution)/shard_map/ppermute | solution.py:253
  30.0 13.1 %collective-permute-done.1 = bf16[32,896]{1,0:T(8,128)(2,1)S(1)} collective-permute-done((bf16[32,896]{1,0:T(8,128)(2,1)S(1)}, bf16[32,896]{1,0:T(8,128)(2,1)S(1)}, u32[]{:S(2)}, u32[]{:S(2)}) %collective-permute-start.1) | collective-permute-done | bytes 57376 | tf_op jit(solution)/shard_map/ppermute | solution.py:253
  43.0 0.0 collective-permute-done.2.refs_5_
  43.0 0.0 collective-permute-done.3.refs_7_
  43.0 0.0 collective-permute-done.4
  43.1 0.0 all-to-all-done
  43.1 0.0 copy-start.4
  43.1 2.3 %fusion.1 = bf16[8,1,56,256]{3,2,0,1:T(8,128)(2,1)S(1)} fusion(bf16[2048,8,56]{0,2,1:T(8,128)(2,1)} %collective-permute-done, bf16[256,2048]{1,0:T(8,128)(2,1)S(1)} %bitcast.42), kind=kOutput, calls=%fused_computation.4 | convolution fusion | flops 469876736 | bytes 3112960 | tf_op jit(solution)/shard_map/tk,kbf->bft/dot_general | solution.py:261
  45.4 0.0 copy-done.4
  45.4 0.7 fusion.18
  46.2 0.0 copy-start.10
  46.2 0.8 copy.29
  47.0 5.4 %all-to-all-start.1 = ((bf16[8,2,56,256]{3,2,1,0:T(8,128)(2,1)}), bf16[8,2,56,256]{3,2,1,0:T(8,128)(2,1)S(1)}, u32[]{:S(2)}, u32[]{:S(2)}) async-start(bf16[8,2,56,256]{3,2,1,0:T(8,128)(2,1)} %copy.29), calls=%async_computation.1 | async-start | bytes 917504 | tf_op jit(solution)/shard_map/all_to_all | solution.py:28
  52.5 0.0 copy-start.5
  52.5 1.5 collective-permute-start.7
  54.0 2.7 %collective-permute-start.6 = (bf16[2,32,896]{2,1,0:T(8,128)(2,1)S(1)}, bf16[2,32,896]{2,1,0:T(8,128)(2,1)S(1)}, u32[]{:S(2)}, u32[]{:S(2)}) collective-permute-start(bf16[2,32,896]{2,1,0:T(8,128)(2,1)S(1)} %pad_maximum_fusion.2.refs_0_), channel_id=1, source_target_pairs={{64,0},{96,32},{0,64},{32,96},{65,1},{97,33},{1,65},{33,97},{66,2}... | collective-permute-start | bytes 344072 | tf_op jit(solution)/shard_map/ppermute | solution.py:270
  56.7 1.5 collective-permute-start.5
  58.1 1.6 %collective-permute-done.7.refs_3_ = bf16[2,32,896]{2,1,0:T(8,128)(2,1)S(1)} collective-permute-done((bf16[2,32,896]{2,1,0:T(8,128)(2,1)S(1)}, bf16[2,32,896]{2,1,0:T(8,128)(2,1)S(1)}, u32[]{:S(2)}, u32[]{:S(2)}) %collective-permute-start.7) | collective-permute-done | bytes 114720 | tf_op jit(solution)/shard_map/ppermute | solution.py:270
  59.8 1.2 collective-permute-done.6.refs_2_
  61.0 0.5 collective-permute-done.5.refs_1_
  61.5 0.0 all-to-all-done.1
  61.5 0.1 reduce_sum.39
  61.6 0.8 broadcast_in_dim.27
  62.4 5.4 %all-to-all-start.2 = ((bf16[8,2,56,256]{3,2,1,0:T(8,128)(2,1)}), bf16[8,2,56,256]{3,2,1,0:T(8,128)(2,1)S(1)}, u32[]{:S(2)}, u32[]{:S(2)}) async-start(bf16[8,2,56,256]{3,2,1,0:T(8,128)(2,1)} %broadcast_in_dim.27), calls=%async_computation.2 | async-start | bytes 917504 | tf_op jit(solution)/shard_map/all_to_all | solution.py:24
  67.8 0.0 copy-done.10
  67.8 0.6 reshape.31.gain
  68.4 0.6 pad_add_fusion.places
  69.0 8.4 %all-to-all-done.2 = bf16[8,2,56,256]{3,2,1,0:T(8,128)(2,1)S(1)} async-done(((bf16[8,2,56,256]{3,2,1,0:T(8,128)(2,1)}), bf16[8,2,56,256]{3,2,1,0:T(8,128)(2,1)S(1)}, u32[]{:S(2)}, u32[]{:S(2)}) %all-to-all-start.2) | async-done | bytes 458784 | tf_op jit(solution)/shard_map/all_to_all | solution.py:24
  77.4 0.0 copy-done.7
  77.4 0.0 copy-done.9
  77.4 0.8 copy-done.1
  78.2 7.2 %expand.1 = bf16[256,4736]{1,0:T(8,128)(2,1)} custom-call(s32[2]{0:T(128)} %pad_add_fusion.places, bf16[896,256]{1,0:T(8,128)(2,1)} %bitcast.44, f32[1,896]{1,0:T(1,128)} %reshape.31.gain, bf16[2,32,896]{2,1,0:T(8,128)(2,1)} %copy-done.5, bf16[2,32,896]{2,1,0:T(8,128)(2,1)} %copy-done.9, bf16[2,32,896]{2,1,0:T(8,128)(2,1)} %copy-done.8, ...), custom_call_target="tpu_custom_call" | custom-call | tf_op jit(solution)/shard_map/expand/pallas_call | solution.py:90
  85.5 32.9 %all_to_all.30 = bf16[8,32,4736]{2,1,0:T(8,128)(2,1)S(1)} all-to-all(bf16[8,32,4736]{2,1,0:T(8,128)(2,1)} %bitcast.39), channel_id=1, replica_groups=mesh['x'=4,'h'=2,'c'=2,'z'=4,'l'=2] {'z','l'}, dimensions={0} | all-to-all | bytes 4849664 | tf_op jit(solution)/shard_map/all_to_all | solution.py:28
  118.4 0.3 convert_reduce_fusion
  118.7 0.1 slice_reduce_fusion
  118.9 0.0 copy-start.3
  118.9 0.2 fusion.12
  119.0 0.1 broadcast_in_dim.30
  119.1 16.7 %all_to_all.31 = bf16[8,32,2304]{2,1,0:T(8,128)(2,1)S(1)} all-to-all(bf16[8,32,2304]{2,1,0:T(8,128)(2,1)S(1)} %broadcast_in_dim.30), channel_id=1, replica_groups=mesh['x'=4,'h'=2,'c'=2,'z'=4,'l'=2] {'z','l'}, dimensions={0} | all-to-all | bytes 2359296 | tf_op jit(solution)/shard_map/all_to_all | solution.py:24
  135.8 0.8 fusion.7
  136.6 3.2 %fusion = bf16[256,896]{1,0:T(8,128)(2,1)} fusion(f32[256,896]{1,0:T(8,128)S(1)} %fusion.7, bf16[1152,896]{1,0:T(8,128)(2,1)} %collective-permute-done.4, bf16[256,2304]{1,0:T(8,128)(2,1)S(1)} %bitcast.41), kind=kOutput, calls=%fused_computation.2 | convolution fusion | flops 528941056 | bytes 4030464 | tf_op jit(solution)/shard_map/dot_general | solution.py:32
  139.9 8.4 %all-to-all-start.5 = ((bf16[8,32,896]{2,1,0:T(8,128)(2,1)}), bf16[8,32,896]{2,1,0:T(8,128)(2,1)S(1)}, u32[]{:S(2)}, u32[]{:S(2)}) async-start(bf16[8,32,896]{2,1,0:T(8,128)(2,1)} %bitcast.17), calls=%async_computation.5 | async-start | bytes 917504 | tf_op jit(solution)/shard_map/all_to_all | solution.py:28
  148.3 9.2 %all-to-all-done.5 = bf16[8,32,896]{2,1,0:T(8,128)(2,1)S(1)} async-done(((bf16[8,32,896]{2,1,0:T(8,128)(2,1)}), bf16[8,32,896]{2,1,0:T(8,128)(2,1)S(1)}, u32[]{:S(2)}, u32[]{:S(2)}) %all-to-all-start.5) | async-done | bytes 458784 | tf_op jit(solution)/shard_map/all_to_all | solution.py:28
  157.5 0.1 convert_reduce_fusion.1
  157.6 0.0 copy-done.2
  157.6 0.9 fusion.4
  (16 shorter events, 0.2 us)
Async XLA Ops:
  0.0 2.0 %copy-start = (bf16[16,128,512]{2,1,0:T(8,128)(2,1)S(1)}, bf16[16,128,512]{2,1,0:T(8,128)(2,1)}, u32[]{:S(2)}) copy-start(bf16[16,128,512]{2,1,0:T(8,128)(2,1)} %param.17) | copy-start | bytes 6291460
  0.0 15.5 %collective-permute-start = (bf16[2048,8,56]{0,2,1:T(8,128)(2,1)}, bf16[2048,8,56]{0,2,1:T(8,128)(2,1)}, u32[]{:S(2)}, u32[]{:S(2)}) collective-permute-start(bf16[2048,8,56]{0,2,1:T(8,128)(2,1)} %param.19), channel_id=1, source_target_pairs={{0,8},{8,0},{1,9},{9,1},{2,10},{10,2},{3,11},{11,3},{4,12},{12,4},... | collective-permute-start | bytes 5505032 | tf_op jit(solution)/shard_map/ppermute | solution.py:36
  0.0 43.0 %collective-permute-start.2 = (bf16[896,1152]{1,0:T(8,128)(2,1)}, bf16[896,1152]{1,0:T(8,128)(2,1)}, u32[]{:S(2)}, u32[]{:S(2)}) collective-permute-start(bf16[896,1152]{1,0:T(8,128)(2,1)} %refs_4_.1), channel_id=1, source_target_pairs={{0,8},{8,0},{1,9},{9,1},{2,10},{10,2},{3,11},{11,3},{4,12},{12,4},... | collective-permute-start | bytes 6193160 | tf_op jit(solution)/shard_map/ppermute | solution.py:36
  0.5 42.5 %collective-permute-start.3 = (bf16[896,1152]{1,0:T(8,128)(2,1)}, bf16[896,1152]{1,0:T(8,128)(2,1)}, u32[]{:S(2)}, u32[]{:S(2)}) collective-permute-start(bf16[896,1152]{1,0:T(8,128)(2,1)} %refs_6_.1), channel_id=1, source_target_pairs={{0,8},{8,0},{1,9},{9,1},{2,10},{10,2},{3,11},{11,3},{4,12},{12,4},... | collective-permute-start | bytes 6193160 | tf_op jit(solution)/shard_map/ppermute | solution.py:36
  0.5 42.5 %collective-permute-start.4 = (bf16[1152,896]{1,0:T(8,128)(2,1)}, bf16[1152,896]{1,0:T(8,128)(2,1)}, u32[]{:S(2)}, u32[]{:S(2)}) collective-permute-start(bf16[1152,896]{1,0:T(8,128)(2,1)} %param.23), channel_id=1, source_target_pairs={{0,8},{8,0},{1,9},{9,1},{2,10},{10,2},{3,11},{11,3},{4,12},{12,4},... | collective-permute-start | bytes 6193160 | tf_op jit(solution)/shard_map/ppermute | solution.py:36
  1.0 1.7 %slice-start = ((bf16[32,16,192]{2,1,0:T(8,128)(2,1)}), bf16[32,16,64]{2,1,0:T(8,128)(2,1)S(1)}, s32[]{:S(2)}) async-start(bf16[32,16,192]{2,1,0:T(8,128)(2,1)} %param.13), calls=%async_computation.6 | async-start | bytes 262144 | tf_op jit(solution)/shard_map/slice | solution.py:214
  17.9 8.5 %copy-start.6 = (bf16[32,896]{1,0:T(8,128)(2,1)S(1)}, bf16[32,896]{1,0:T(8,128)(2,1)}, u32[]{:S(2)}) copy-start(bf16[32,896]{1,0:T(8,128)(2,1)} %param.12) | copy-start | bytes 172036
  19.1 23.9 %all-to-all-start = ((bf16[8,32,2048]{2,1,0:T(8,128)(2,1)}), bf16[8,32,2048]{2,1,0:T(8,128)(2,1)S(1)}, u32[]{:S(2)}, u32[]{:S(2)}) async-start(bf16[8,32,2048]{2,1,0:T(8,128)(2,1)} %broadcast_in_dim.26), calls=%async_computation | async-start | bytes 2097152 | tf_op jit(solution)/shard_map/all_to_all | solution.py:24
  26.5 16.6 %collective-permute-start.1 = (bf16[32,896]{1,0:T(8,128)(2,1)S(1)}, bf16[32,896]{1,0:T(8,128)(2,1)S(1)}, u32[]{:S(2)}, u32[]{:S(2)}) collective-permute-start(bf16[32,896]{1,0:T(8,128)(2,1)S(1)} %copy-done.6), channel_id=1, source_target_pairs={{0,16},{16,0},{1,17},{17,1},{2,18},{18,2},{3,19},{19,3},{4,20},{20... | collective-permute-start | bytes 172040 | tf_op jit(solution)/shard_map/ppermute | solution.py:253
  43.1 2.3 %copy-start.4 = (bf16[2048,8,56]{0,2,1:T(8,128)(2,1)S(1)}, bf16[2048,8,56]{0,2,1:T(8,128)(2,1)}, u32[]{:S(2)}) copy-start(bf16[2048,8,56]{0,2,1:T(8,128)(2,1)} %param.19) | copy-start | bytes 5505028
  46.2 21.6 %copy-start.10 = (bf16[896]{0:T(1024)(128)(2,1)S(1)}, bf16[896]{0:T(1024)(128)(2,1)}, u32[]{:S(2)}) copy-start(bf16[896]{0:T(1024)(128)(2,1)} %param.20) | copy-start | bytes 5380
  47.0 14.5 %all-to-all-start.1 = ((bf16[8,2,56,256]{3,2,1,0:T(8,128)(2,1)}), bf16[8,2,56,256]{3,2,1,0:T(8,128)(2,1)S(1)}, u32[]{:S(2)}, u32[]{:S(2)}) async-start(bf16[8,2,56,256]{3,2,1,0:T(8,128)(2,1)} %copy.29), calls=%async_computation.1 | async-start | bytes 917504 | tf_op jit(solution)/shard_map/all_to_all | solution.py:28
  52.5 24.9 %copy-start.5 = (bf16[2,32,896]{2,1,0:T(8,128)(2,1)}, bf16[2,32,896]{2,1,0:T(8,128)(2,1)S(1)}, u32[]{:S(2)}) copy-start(bf16[2,32,896]{2,1,0:T(8,128)(2,1)S(1)} %pad_maximum_fusion.2.refs_0_) | copy-start | bytes 344068
  52.5 7.3 %collective-permute-start.7 = (bf16[2,32,896]{2,1,0:T(8,128)(2,1)S(1)}, bf16[2,32,896]{2,1,0:T(8,128)(2,1)S(1)}, u32[]{:S(2)}, u32[]{:S(2)}) collective-permute-start(bf16[2,32,896]{2,1,0:T(8,128)(2,1)S(1)} %pad_maximum_fusion.2.refs_0_), channel_id=1, source_target_pairs={{96,0},{0,32},{32,64},{64,96},{97,1},{1,33},{33,65},{65,97},{98,2}... | collective-permute-start | bytes 344072 | tf_op jit(solution)/shard_map/ppermute | solution.py:270
  54.0 7.0 %collective-permute-start.6 = (bf16[2,32,896]{2,1,0:T(8,128)(2,1)S(1)}, bf16[2,32,896]{2,1,0:T(8,128)(2,1)S(1)}, u32[]{:S(2)}, u32[]{:S(2)}) collective-permute-start(bf16[2,32,896]{2,1,0:T(8,128)(2,1)S(1)} %pad_maximum_fusion.2.refs_0_), channel_id=1, source_target_pairs={{64,0},{96,32},{0,64},{32,96},{65,1},{97,33},{1,65},{33,97},{66,2}... | collective-permute-start | bytes 344072 | tf_op jit(solution)/shard_map/ppermute | solution.py:270
  56.7 4.8 %collective-permute-start.5 = (bf16[2,32,896]{2,1,0:T(8,128)(2,1)S(1)}, bf16[2,32,896]{2,1,0:T(8,128)(2,1)S(1)}, u32[]{:S(2)}, u32[]{:S(2)}) collective-permute-start(bf16[2,32,896]{2,1,0:T(8,128)(2,1)S(1)} %pad_maximum_fusion.2.refs_0_), channel_id=1, source_target_pairs={{32,0},{64,32},{96,64},{0,96},{33,1},{65,33},{97,65},{1,97},{34,2}... | collective-permute-start | bytes 344072 | tf_op jit(solution)/shard_map/ppermute | solution.py:270
  59.8 17.6 %copy-start.7 = (bf16[2,32,896]{2,1,0:T(8,128)(2,1)}, bf16[2,32,896]{2,1,0:T(8,128)(2,1)S(1)}, u32[]{:S(2)}) copy-start(bf16[2,32,896]{2,1,0:T(8,128)(2,1)S(1)} %collective-permute-done.7.refs_3_) | copy-start | bytes 344068
  61.0 16.4 %copy-start.8 = (bf16[2,32,896]{2,1,0:T(8,128)(2,1)}, bf16[2,32,896]{2,1,0:T(8,128)(2,1)S(1)}, u32[]{:S(2)}) copy-start(bf16[2,32,896]{2,1,0:T(8,128)(2,1)S(1)} %collective-permute-done.6.refs_2_) | copy-start | bytes 344068
  61.5 15.9 %copy-start.9 = (bf16[2,32,896]{2,1,0:T(8,128)(2,1)}, bf16[2,32,896]{2,1,0:T(8,128)(2,1)S(1)}, u32[]{:S(2)}) copy-start(bf16[2,32,896]{2,1,0:T(8,128)(2,1)S(1)} %collective-permute-done.5.refs_1_) | copy-start | bytes 344068
  62.4 15.0 %all-to-all-start.2 = ((bf16[8,2,56,256]{3,2,1,0:T(8,128)(2,1)}), bf16[8,2,56,256]{3,2,1,0:T(8,128)(2,1)S(1)}, u32[]{:S(2)}, u32[]{:S(2)}) async-start(bf16[8,2,56,256]{3,2,1,0:T(8,128)(2,1)} %broadcast_in_dim.27), calls=%async_computation.2 | async-start | bytes 917504 | tf_op jit(solution)/shard_map/all_to_all | solution.py:24
  77.4 0.8 copy-start.1
  118.9 16.9 %copy-start.3 = (bf16[1152,896]{1,0:T(8,128)(2,1)S(1)}, bf16[1152,896]{1,0:T(8,128)(2,1)}, u32[]{:S(2)}) copy-start(bf16[1152,896]{1,0:T(8,128)(2,1)} %param.23) | copy-start | bytes 6193156
  136.6 21.0 %copy-start.2 = (bf16[8,2,56,256]{3,2,1,0:T(8,128)(2,1)S(1)}, bf16[8,2,56,256]{3,2,1,0:T(8,128)(2,1)}, u32[]{:S(2)}) copy-start(bf16[8,2,56,256]{3,2,1,0:T(8,128)(2,1)} %copy-done.1) | copy-start | bytes 1376260
  139.9 17.7 %all-to-all-start.5 = ((bf16[8,32,896]{2,1,0:T(8,128)(2,1)}), bf16[8,32,896]{2,1,0:T(8,128)(2,1)S(1)}, u32[]{:S(2)}, u32[]{:S(2)}) async-start(bf16[8,32,896]{2,1,0:T(8,128)(2,1)} %bitcast.17), calls=%async_computation.5 | async-start | bytes 917504 | tf_op jit(solution)/shard_map/all_to_all | solution.py:28

commit v4 on v3

--- a/solution.py
+++ b/solution.py
@@ -47,16 +47,22 @@
 
     def kernel(places, attention_out, gain, *refs):
         pieces, sources = refs[:steps], refs[steps : steps + len(weights)]
-        out, ready, slots, sums, power_slot, sems = refs[steps + len(weights) :]
+        out, ready, across_slot, slots, sums, power_slot, sems = refs[steps + len(weights) :]
 
         def copy(i, source, target):
             return pltpu.make_async_copy(source, target, sems.at[i])
 
         first = [copy(i, piece, ready.at[i]) for i, piece in enumerate(pieces)]
-        second = [copy(steps + i, w, slots.at[i]) for i, w in enumerate(sources)]
-        for c in first + second:
+        first.append(copy(steps, attention_out, across_slot))
+        second = [
+            copy(steps + 1 + 2 * i + j, w.at[half], slots.at[i, half])
+            for i, w in enumerate(sources)
+            for j, half in enumerate((slice(0, width // 2), slice(width // 2, width)))
+        ]
+        for c in first + second[:4]:
             c.start()
-        across = attention_out[...].T.astype(F32)
+        first.pop().wait()
+        across = across_slot[...].T.astype(F32)
         for c in first:
             c.wait()
         blocks = []
@@ -75,12 +81,15 @@
         lane = lax.broadcasted_iota(jnp.int32, (tokens, LANES), 1)
         parts = jnp.where(lane == 0, high, jnp.where(lane == 1, middle, low))
         power_slot[...] = jnp.where(lane < 3, parts, 0.0).astype(BF16)
-        base = steps + len(weights)
+        base = steps + 1 + 2 * len(weights)
         last = [copy(base, power_slot, out.at[:, len(weights) * units :])]
         last[0].start()
         scaled = (hidden * gain[...]).astype(BF16)
-        for i, c in enumerate(second):
-            c.wait()
+        for i in range(len(weights)):
+            for c in second[2 * i : 2 * i + 2]:
+                c.wait()
+            for c in second[2 * i + 4 : 2 * i + 6]:
+                c.start()
             sums[i] = dot(scaled, slots[i], ((1,), (0,))).astype(BF16)
             last.append(copy(base + 1 + i, sums.at[i], out.at[:, i * units : (i + 1) * units]))
             last[-1].start()
@@ -89,28 +98,34 @@
 
     return pl.pallas_call(
         kernel,
-        in_specs=[pl.BlockSpec(memory_space=pltpu.SMEM), VMEM, VMEM]
+        in_specs=[pl.BlockSpec(memory_space=pltpu.SMEM), HBM, VMEM]
         + [HBM] * (steps + len(weights)),
         out_specs=HBM,
         out_shape=jax.ShapeDtypeStruct((tokens, len(weights) * units + LANES), BF16),
         scratch_shapes=[
             pltpu.VMEM((steps, sides, rows, width), BF16),
+            pltpu.VMEM((width, tokens), BF16),
             pltpu.VMEM((len(weights), width, units), BF16),
             pltpu.VMEM((len(weights), tokens, units), BF16),
             pltpu.VMEM((tokens, LANES), BF16),
-            pltpu.SemaphoreType.DMA((steps + 2 * len(weights) + 1,)),
+            pltpu.SemaphoreType.DMA((steps + 2 + 3 * len(weights),)),
         ],
         name="expand",
     )(places, attention_cols, gain, *residuals, *weights)
 
 
-def attend(lengths, query_full, new_latent, cache_cols, latent_width, softmax_scale):
-    samples, heads, entry = query_full.shape
-    slots = cache_cols.shape[2]
+def attend(lengths, query_latent, queries, new_latent, cache_cols, w_value, copies_out):
+    samples, heads, latent_width = query_latent.shape
+    entry, slots = cache_cols.shape[1:]
+    value_width = w_value.shape[2]
+    nope_width = queries.shape[2] - (entry - latent_width)
+    softmax_scale = 1.0 / math.sqrt(queries.shape[2])
     blocks = slots // LANES
     groups = samples // GROUP
 
-    def kernel(lengths, query, new, cache, out, buf, fresh, order, sems):
+    def kernel(
+        lengths, latent, query, new, cache, w, out, buf, fresh, mixed, w_slot, values, order, sems, w_sem
+    ):
         def live(s):
             return lax.div(lengths[s] + (LANES - 1), LANES)
 
@@ -151,6 +166,8 @@
         wait = functools.partial(copies, lambda copy: copy.wait())
         by_size(0, start)
         by_size(1, start)
+        w_copy = pltpu.make_async_copy(w, w_slot, w_sem.at[0])
+        w_copy.start()
         for s in range(samples):
             fresh[s] = new[s : s + 1, :].astype(F32)
 
@@ -159,11 +176,20 @@
             scores, own = [], []
             for g in range(GROUP):
                 s = order[i * GROUP + g]
-                q = query[s]
-                part = dot(q, buf[half + g, :, :size], ((1,), (0,))) * softmax_scale
+                q = latent[s]
+                turned = query[s][:, nope_width:]
+                part = dot(q, buf[half + g, :latent_width, :size], ((1,), (0,)))
+                part = part + dot(turned, buf[half + g, latent_width:, :size], ((1,), (0,)))
+                part = part * softmax_scale
                 positions = lax.broadcasted_iota(jnp.int32, part.shape, 1)
                 scores.append(jnp.where(positions < lengths[s], part, -1e30))
-                own.append(jnp.sum(q.astype(F32) * fresh[s], axis=1, keepdims=True))
+                fresh_row = fresh[s]
+                own.append(
+                    jnp.sum(q.astype(F32) * fresh_row[:, :latent_width], axis=1, keepdims=True)
+                    + jnp.sum(
+                        turned.astype(F32) * fresh_row[:, latent_width:], axis=1, keepdims=True
+                    )
+                )
             scores = jnp.concatenate(scores, axis=0)
             own = jnp.concatenate(own, axis=0) * softmax_scale
             peak = jnp.maximum(jnp.max(scores, axis=1, keepdims=True), own)
@@ -175,9 +201,9 @@
             for g in range(GROUP):
                 s = order[i * GROUP + g]
                 mine = slice(g * heads, (g + 1) * heads)
-                values = buf[half + g, :latent_width, :size]
-                mixed = dot(values, probs[mine], ((1,), (1,))).T
-                out[s] = (mixed + own_prob[mine] * fresh[s][:, :latent_width]).astype(BF16)
+                kept = buf[half + g, :latent_width, :size]
+                sums = dot(kept, probs[mine], ((1,), (1,))).T
+                mixed[:, i, g, :] = sums + own_prob[mine] * fresh[s][:, :latent_width]
 
         def step(i, carry):
             by_size(i, wait)
@@ -191,35 +217,49 @@
 
         lax.fori_loop(0, groups, step, 0)
 
+        row = lax.broadcasted_iota(jnp.int32, (samples, samples), 0)
+        col = lax.broadcasted_iota(jnp.int32, (samples, samples), 1)
+        source = jnp.zeros((samples, samples), jnp.int32)
+        for p in range(samples):
+            source = jnp.where(col == p, order[p], source)
+        back = (source == row).astype(BF16)
+        w_copy.wait()
+        heads_values = [
+            dot(mixed[h].reshape(samples, latent_width).astype(BF16), w_slot[h], ((1,), (0,)))
+            for h in range(heads)
+        ]
+        sorted_values = jnp.concatenate(heads_values, axis=1).astype(BF16)
+        values[...] = dot(back, sorted_values, ((1,), (0,))).astype(BF16)
+        last = [
+            pltpu.make_async_copy(values, out.at[i], sems.at[i]) for i in range(copies_out)
+        ]
+        for c in last:
+            c.start()
+        for c in last:
+            c.wait()
+
     return pl.pallas_call(
         kernel,
-        in_specs=[pl.BlockSpec(memory_space=pltpu.SMEM), VMEM, VMEM, HBM],
-        out_specs=VMEM,
-        out_shape=jax.ShapeDtypeStruct((samples, heads, latent_width), BF16),
+        in_specs=[pl.BlockSpec(memory_space=pltpu.SMEM), VMEM, VMEM, VMEM, HBM, HBM],
+        out_specs=HBM,
+        out_shape=jax.ShapeDtypeStruct((copies_out, samples, heads * value_width), BF16),
         scratch_shapes=[
             pltpu.VMEM((2 * GROUP, entry, slots), BF16),
             pltpu.VMEM((samples, 1, entry), F32),
+            pltpu.VMEM((heads, groups, GROUP, latent_width), F32),
+            pltpu.VMEM(w_value.shape, BF16),
+            pltpu.VMEM((samples, heads * value_width), BF16),
             pltpu.SMEM((samples,), jnp.int32),
             pltpu.SemaphoreType.DMA((2 * GROUP,)),
+            pltpu.SemaphoreType.DMA((1,)),
         ],
+        cost_estimate=pl.CostEstimate(
+            flops=4 * samples * heads * slots * entry,
+            bytes_accessed=2 * samples * slots * entry,
+            transcendentals=samples * heads * slots,
+        ),
         name="attend",
-    )(lengths, query_full, new_latent, cache_cols)
-
-
-def attention(queries, latent_cache, new_latent, lengths, w_absorb):
-    nope_width = w_absorb.shape[1]
-    query_latent = jnp.einsum(
-        "shn,hnc->shc", queries[:, :, :nope_width], w_absorb, preferred_element_type=F32
-    ).astype(BF16)
-    query_full = jnp.concatenate([query_latent, queries[:, :, nope_width:]], axis=2)
-    return attend(
-        lengths,
-        query_full,
-        new_latent,
-        latent_cache.swapaxes(1, 2),
-        w_absorb.shape[2],
-        1.0 / math.sqrt(queries.shape[2]),
-    )
+    )(lengths, query_latent, queries, new_latent, cache_cols, w_value)
 
 
 def layer(
@@ -245,24 +285,33 @@
     w_up_other = other_core(w_up)
     w_down_other = other_core(w_down)
 
-    head_latent = attention(queries, latent_cache, new_latent, lengths, w_absorb)
-    head_latent, w_out_other = lax.optimization_barrier((head_latent, w_out_other))
-    head_values = jnp.einsum("shc,hcv->shv", head_latent, w_value, preferred_element_type=F32)
-    head_values = head_values.astype(BF16).reshape(rows, -1)
-    all_values = from_everyone(head_values, CHIPS).reshape(-1, head_values.shape[1])
+    query_latent = jnp.einsum(
+        "shn,hnc->shc", queries[:, :, : w_absorb.shape[1]], w_absorb, preferred_element_type=F32
+    ).astype(BF16)
+    head_values = attend(
+        lengths,
+        query_latent,
+        queries,
+        new_latent,
+        latent_cache.swapaxes(1, 2),
+        w_value,
+        lax.axis_size(CHIPS),
+    )
+    head_values, w_out_other = lax.optimization_barrier((head_values, w_out_other))
+    w_out_both = jnp.stack([w_out, w_out_other], axis=2)
+    all_values = exchange(head_values, CHIPS).reshape(-1, head_values.shape[2])
     across = lax.ppermute(residual, "h", [(0, 1), (1, 0)])
-    all_values, across, w_gate_other, w_up_other, w_down_other = lax.optimization_barrier(
-        (all_values, across, w_gate_other, w_up_other, w_down_other)
-    )
+    all_values, across, w_out_both, w_gate_other, w_up_other, w_down_other = (
+        lax.optimization_barrier(
+            (all_values, across, w_out_both, w_gate_other, w_up_other, w_down_other)
+        )
+    )
+    w_down_both = jnp.concatenate([w_down, w_down_other], axis=0)
     tokens = all_values.shape[0]
 
-    partial = jnp.stack(
-        [
-            jnp.einsum("tk,kbf->bft", all_values, w, preferred_element_type=F32).astype(BF16)
-            for w in (w_out, w_out_other)
-        ],
-        axis=1,
-    )
+    partial = jnp.einsum(
+        "tk,kbcf->bcft", all_values, w_out_both, preferred_element_type=F32
+    ).astype(BF16)
     arrived = exchange(partial, HP)
     both_rows = jnp.stack([residual, across])
     steps = lax.axis_size("x")
@@ -270,7 +319,9 @@
         lax.ppermute(both_rows, "x", [((i + step) % steps, i) for i in range(steps)])
         for step in range(1, steps)
     ]
-    arrived, *residuals = lax.optimization_barrier((arrived, *residuals))
+    arrived, w_down_both, *residuals = lax.optimization_barrier(
+        (arrived, w_down_both, *residuals)
+    )
     summed = arrived.astype(F32).sum(axis=0).astype(BF16)
     summed = jnp.where(core == 0, summed, summed[::-1])
     attention_cols = from_everyone(summed, CHIPS).reshape(width, tokens)
@@ -292,11 +343,7 @@
     share = (jax.nn.silu(gate_sum) * up_sum).astype(BF16)
     activated = from_everyone(share, HP).reshape(tokens, -1)
 
-    own_units = w_down.shape[0]
-    ffn = sum(
-        dot(activated[:, i * own_units : (i + 1) * own_units], w, ((1,), (0,)))
-        for i, w in enumerate((w_down, w_down_other))
-    ).astype(BF16)
+    ffn = dot(activated, w_down_both, ((1,), (0,))).astype(BF16)
     ffn = exchange(ffn.reshape(-1, rows, width), CHIPS).astype(F32).sum(axis=0)
 
     pick = (

time: 159 us -> 151 us (0.950)
  other arithmetic: 2.39 us -> 10 us
  starting transfers between devices: 36.8 us -> 30.4 us
  waiting for transfers between devices: 34.1 us -> 30 us
  matrix products: 10.7 us -> 7.43 us
    all_to_all x2 -> x1, starting transfers between devices: 12.7 us -> 3.65 us  [from_everyone(): lax.all_to_all(jnp.broadcast_to(x[None], (devices, *x.shape)), axes, 0, 0...]
    ppermute x1, waiting for transfers between devices: 13.1 us -> 8.76 us  [layer(): across = lax.ppermute(residual, 'h', [(0, 1), (1, 0)])]
    all_to_all x2 -> x3, waiting for transfers between devices: 9.24 us -> 13.5 us  [exchange(): return lax.all_to_all(x, axes, 0, 0, tiled=True)]
    another operation x2 -> x1, other arithmetic: 0.07 us -> 4.2 us  [layer(): w_out_both = jnp.stack([w_out, w_out_other], axis=2)]
    concatenate x1, other arithmetic: 0.94 us -> 4.47 us  [layer(): w_down_both = jnp.concatenate([w_down, w_down_other], axis=0)]
    ppermute x3, waiting for transfers between devices: 3.32 us -> 0.01 us  [layer(): lax.ppermute(both_rows, 'x', [((i + step) % steps, i) for i in range(step...]
    all_to_all x2 -> x3, starting transfers between devices: 13.9 us -> 16.5 us  [exchange(): return lax.all_to_all(x, axes, 0, 0, tiled=True)]
    dot_general x3 -> x2, matrix products: 4.93 us -> 3.05 us  [dot(): return lax.dot_general(a, b, (dims, ((), ())), preferred_element_type=F32)]
  transfers between devices with their start and end apart: 12 -> 12, of which waited for: 6 -> 4; matrix products, arithmetic and copies ran while one was open for 5% -> 11% of each run, Pallas kernels for 8% -> 9%
where the time goes in v4:
time: 151 us
  blocking collectives  48.2 us (32%)
  starting transfers between devices  30.4 us (20%)
  waiting for transfers between devices  30 us (20%)
  Pallas kernels  20.1 us (13%)
  other arithmetic  10 us (7%)
  matrix products  7.43 us (5%)
  local copies, waits for them, and re-layouts  4.29 us (3%)
    all_to_all x1, blocking collectives, exchange(): return lax.all_to_all(x, axes, 0, 0, tiled=True)  31.7 us
    all_to_all x1, blocking collectives, from_everyone(): lax.all_to_all(jnp.broadcast_to(x[None], (devices, *x.shape)), axes, 0, 0...  16.5 us
    all_to_all x3, starting transfers between devices, exchange(): return lax.all_to_all(x, axes, 0, 0, tiled=True)  16.5 us
    all_to_all x3, waiting for transfers between devices, exchange(): return lax.all_to_all(x, axes, 0, 0, tiled=True)  13.5 us
    pallas_call x1, Pallas kernels, attend(): pl.pallas_call(kernel, in_specs=[pl.BlockSpec(memory_space=pltpu.SMEM), V...  12.8 us
    ppermute x1, waiting for transfers between devices, layer(): across = lax.ppermute(residual, 'h', [(0, 1), (1, 0)])  8.76 us
    all_to_all x1, waiting for transfers between devices, from_everyone(): lax.all_to_all(jnp.broadcast_to(x[None], (devices, *x.shape)), axes, 0, 0...  7.78 us
    pallas_call x1, Pallas kernels, expand(): pl.pallas_call(kernel, in_specs=[pl.BlockSpec(memory_space=pltpu.SMEM), H...  7.27 us
  transfers between devices with their start and end apart: 12, of which 4 were waited for; matrix products, arithmetic and copies ran while one was open for 11% of the time, Pallas kernels for 9%

profile of v4, /device:TPU:0, one launch (start us, length us, event | category | flops | bytes accessed | tf_op | source)
XLA Modules:
  0.0 150.7 jit_solution(7820949783898726396)
XLA Ops:
  0.0 0.0 copy-start
  0.0 0.0 collective-permute-start
  0.0 0.5 collective-permute-start.2
  0.5 0.0 collective-permute-start.3
  0.5 0.5 collective-permute-start.4
  1.0 0.9 slice.12
  1.9 0.0 copy-done
  2.0 0.4 fusion.11
  2.4 1.1 copy.30
  3.5 0.0 copy-start.5
  3.5 12.8 %attend.1 = bf16[8,32,2048]{2,1,0:T(8,128)(2,1)} custom-call(s32[32]{0:T(128)} %lengths.1, bf16[32,16,512]{2,1,0:T(8,128)(2,1)} %bitcast.28, bf16[32,16,192]{2,1,0:T(8,128)(2,1)} %query.1, bf16[32,576]{1,0:T(8,128)(2,1)} %new.1, bf16[32,576,512]{2,1,0:T(8,128)(2,1)} %bitcast.24, bf16[16,512,128]{2,1,0:T(8,128)(2,1)} %w.1), custom_call_target="tpu_custom_call" | custom-call | flops 603979776 | bytes 18874368 | tf_op jit(solution)/shard_map/attend/pallas_call | solution.py:241
  16.3 0.0 collective-permute-done
  16.3 7.4 %all-to-all-start = ((bf16[8,32,2048]{2,1,0:T(8,128)(2,1)}), bf16[8,32,2048]{2,1,0:T(8,128)(2,1)S(1)}, u32[]{:S(2)}, u32[]{:S(2)}) async-start(bf16[8,32,2048]{2,1,0:T(8,128)(2,1)} %attend.1), calls=%async_computation | async-start | bytes 2097152 | tf_op jit(solution)/shard_map/all_to_all | solution.py:28
  23.7 0.0 copy-done.5
  23.7 3.5 %collective-permute-start.1 = (bf16[32,896]{1,0:T(8,128)(2,1)S(1)}, bf16[32,896]{1,0:T(8,128)(2,1)S(1)}, u32[]{:S(2)}, u32[]{:S(2)}) collective-permute-start(bf16[32,896]{1,0:T(8,128)(2,1)S(1)} %copy-done.5), channel_id=1, source_target_pairs={{0,16},{16,0},{1,17},{17,1},{2,18},{18,2},{3,19},{19,3},{4,20},{20... | collective-permute-start | bytes 172040 | tf_op jit(solution)/shard_map/ppermute | solution.py:303
  27.2 4.2 %pad_maximum_fusion.1 = bf16[2048,8,2,56]{0,3,1,2:T(8,128)(2,1)} fusion(bf16[2048,8,1,56]{0,3,1,2:T(8,128)(2,1)} %bitcast.4, bf16[2048,8,1,56]{0,3,1,2:T(8,128)(2,1)} %bitcast.29), kind=kLoop, calls=%fused_computation.2 | loop fusion | flops 1835008 | bytes 7340032 | tf_op jit(solution)/shard_map/stack | solution.py:301
  31.4 8.8 %collective-permute-done.1 = bf16[32,896]{1,0:T(8,128)(2,1)S(1)} collective-permute-done((bf16[32,896]{1,0:T(8,128)(2,1)S(1)}, bf16[32,896]{1,0:T(8,128)(2,1)S(1)}, u32[]{:S(2)}, u32[]{:S(2)}) %collective-permute-start.1) | collective-permute-done | bytes 57376 | tf_op jit(solution)/shard_map/ppermute | solution.py:303
  40.2 0.0 collective-permute-done.2.refs_5_
  40.2 0.0 collective-permute-done.3.refs_7_
  40.2 0.0 collective-permute-done.4
  40.2 0.0 all-to-all-done
  40.3 0.0 copy-start.4
  40.3 1.5 %collective-permute-start.7 = (bf16[2,32,896]{2,1,0:T(8,128)(2,1)S(1)}, bf16[2,32,896]{2,1,0:T(8,128)(2,1)S(1)}, u32[]{:S(2)}, u32[]{:S(2)}) collective-permute-start(bf16[2,32,896]{2,1,0:T(8,128)(2,1)S(1)} %pad_maximum_fusion.2.refs_0_), channel_id=1, source_target_pairs={{96,0},{0,32},{32,64},{64,96},{97,1},{1,33},{33,65},{65,97},{98,2}... | collective-permute-start | bytes 344072 | tf_op jit(solution)/shard_map/ppermute | solution.py:319
  41.8 2.7 %collective-permute-start.6 = (bf16[2,32,896]{2,1,0:T(8,128)(2,1)S(1)}, bf16[2,32,896]{2,1,0:T(8,128)(2,1)S(1)}, u32[]{:S(2)}, u32[]{:S(2)}) collective-permute-start(bf16[2,32,896]{2,1,0:T(8,128)(2,1)S(1)} %pad_maximum_fusion.2.refs_0_), channel_id=1, source_target_pairs={{64,0},{96,32},{0,64},{32,96},{65,1},{97,33},{1,65},{33,97},{66,2}... | collective-permute-start | bytes 344072 | tf_op jit(solution)/shard_map/ppermute | solution.py:319
  44.5 1.5 collective-permute-start.5
  45.9 4.0 %fusion.2 = bf16[8,2,56,256]{3,2,1,0:T(8,128)(2,1)} fusion(bf16[2048,8,2,56]{0,3,1,2:T(8,128)(2,1)} %pad_maximum_fusion.1, bf16[256,2048]{1,0:T(8,128)(2,1)S(1)} %bitcast.31), kind=kOutput, calls=%fused_computation.6 | convolution fusion | flops 939753472 | bytes 5177344 | tf_op jit(solution)/shard_map/tk,kbcf->bcft/dot_general | solution.py:312
  49.9 0.0 copy-done.4
  49.9 5.4 %all-to-all-start.1 = ((bf16[8,2,56,256]{3,2,1,0:T(8,128)(2,1)}), bf16[8,2,56,256]{3,2,1,0:T(8,128)(2,1)S(1)}, u32[]{:S(2)}, u32[]{:S(2)}) async-start(bf16[8,2,56,256]{3,2,1,0:T(8,128)(2,1)} %fusion.2), calls=%async_computation.1 | async-start | bytes 917504 | tf_op jit(solution)/shard_map/all_to_all | solution.py:28
  55.3 0.0 copy-start.8
  55.4 4.5 %pad_maximum_fusion = bf16[2304,896]{1,0:T(8,128)(2,1)} fusion(bf16[1152,896]{1,0:T(8,128)(2,1)} %collective-permute-done.4, bf16[1152,896]{1,0:T(8,128)(2,1)} %param.23), kind=kLoop, calls=%fused_computation.1 | loop fusion | flops 8257536 | bytes 8257536 | tf_op jit(solution)/shard_map/concatenate | solution.py:309
  59.8 0.0 collective-permute-done.7.refs_3_
  59.8 0.0 copy-start.6
  59.8 0.0 collective-permute-done.6.refs_2_
  59.8 0.0 copy-start.7
  59.8 0.0 collective-permute-done.5.refs_1_
  59.8 4.2 %all-to-all-done.1 = bf16[8,2,56,256]{3,2,1,0:T(8,128)(2,1)S(1)} async-done(((bf16[8,2,56,256]{3,2,1,0:T(8,128)(2,1)}), bf16[8,2,56,256]{3,2,1,0:T(8,128)(2,1)S(1)}, u32[]{:S(2)}, u32[]{:S(2)}) %all-to-all-start.1) | async-done | bytes 458784 | tf_op jit(solution)/shard_map/all_to_all | solution.py:28
  64.1 0.1 reduce_sum.39
  64.2 0.8 broadcast_in_dim.8
  65.0 3.7 %all-to-all-start.2 = ((bf16[8,2,56,256]{3,2,1,0:T(8,128)(2,1)}), bf16[8,2,56,256]{3,2,1,0:T(8,128)(2,1)S(1)}, u32[]{:S(2)}, u32[]{:S(2)}) async-start(bf16[8,2,56,256]{3,2,1,0:T(8,128)(2,1)} %broadcast_in_dim.8), calls=%async_computation.2 | async-start | bytes 917504 | tf_op jit(solution)/shard_map/all_to_all | solution.py:24
  68.6 0.0 copy-done.8
  68.7 0.6 reshape.30.gain
  69.2 0.6 pad_add_fusion.places
  69.8 7.8 %all-to-all-done.2 = bf16[8,2,56,256]{3,2,1,0:T(8,128)(2,1)S(1)} async-done(((bf16[8,2,56,256]{3,2,1,0:T(8,128)(2,1)}), bf16[8,2,56,256]{3,2,1,0:T(8,128)(2,1)S(1)}, u32[]{:S(2)}, u32[]{:S(2)}) %all-to-all-start.2) | async-done | bytes 458784 | tf_op jit(solution)/shard_map/all_to_all | solution.py:24
  77.6 0.0 copy-start.2
  77.6 0.0 copy-done.6
  77.6 0.0 copy-done.7
  77.6 0.8 copy-done.2
  78.4 7.3 %expand.1 = bf16[256,4736]{1,0:T(8,128)(2,1)} custom-call(s32[2]{0:T(128)} %pad_add_fusion.places, bf16[896,256]{1,0:T(8,128)(2,1)} %bitcast.26, f32[1,896]{1,0:T(1,128)} %reshape.30.gain, bf16[2,32,896]{2,1,0:T(8,128)(2,1)} %copy-done.4, bf16[2,32,896]{2,1,0:T(8,128)(2,1)} %collective-permute-done.5.refs_1_, bf16[2,32,896]{2,1,0:T(8,128)(2,1)} %copy-done.7, ...), custom_call_target="tpu_custom_call" | custom-call | tf_op jit(solution)/shard_map/expand/pallas_call | solution.py:99
  85.7 31.7 %all_to_all.30 = bf16[8,32,4736]{2,1,0:T(8,128)(2,1)S(1)} all-to-all(bf16[8,32,4736]{2,1,0:T(8,128)(2,1)} %bitcast.25), channel_id=1, replica_groups=mesh['x'=4,'h'=2,'c'=2,'z'=4,'l'=2] {'z','l'}, dimensions={0} | all-to-all | bytes 4849664 | tf_op jit(solution)/shard_map/all_to_all | solution.py:28
  117.3 0.3 convert_reduce_fusion
  117.7 0.0 copy-start.1
  117.7 0.1 slice_reduce_fusion
  117.8 0.2 fusion.10
  118.0 0.1 broadcast_in_dim.21
  118.1 16.5 %all_to_all.31 = bf16[8,32,2304]{2,1,0:T(8,128)(2,1)S(1)} all-to-all(bf16[8,32,2304]{2,1,0:T(8,128)(2,1)S(1)} %broadcast_in_dim.21), channel_id=1, replica_groups=mesh['x'=4,'h'=2,'c'=2,'z'=4,'l'=2] {'z','l'}, dimensions={0} | all-to-all | bytes 2359296 | tf_op jit(solution)/shard_map/all_to_all | solution.py:24
  134.6 0.0 copy-done.1
  134.6 0.0 copy-start.3
  134.6 2.2 %convolution_convert_fusion = bf16[256,896]{1,0:T(8,128)(2,1)} fusion(bf16[256,2304]{1,0:T(8,128)(2,1)S(1)} %bitcast.30, bf16[2304,896]{1,0:T(8,128)(2,1)S(1)} %copy-done.1), kind=kOutput, calls=%fused_computation.5 | convolution fusion | flops 1057193984 | bytes 5767168 | tf_op jit(solution)/shard_map/dot_general | solution.py:32
  136.8 3.7 %all-to-all-start.5 = ((bf16[8,32,896]{2,1,0:T(8,128)(2,1)}), bf16[8,32,896]{2,1,0:T(8,128)(2,1)S(1)}, u32[]{:S(2)}, u32[]{:S(2)}) async-start(bf16[8,32,896]{2,1,0:T(8,128)(2,1)} %bitcast.14), calls=%async_computation.5 | async-start | bytes 917504 | tf_op jit(solution)/shard_map/all_to_all | solution.py:28
  140.5 9.2 %all-to-all-done.5 = bf16[8,32,896]{2,1,0:T(8,128)(2,1)S(1)} async-done(((bf16[8,32,896]{2,1,0:T(8,128)(2,1)}), bf16[8,32,896]{2,1,0:T(8,128)(2,1)S(1)}, u32[]{:S(2)}, u32[]{:S(2)}) %all-to-all-start.5) | async-done | bytes 458784 | tf_op jit(solution)/shard_map/all_to_all | solution.py:28
  149.7 0.1 convert_reduce_fusion.1
  149.8 0.0 copy-done.3
  149.8 0.9 fusion.6
  (4 shorter events, 0.0 us)
Async XLA Ops:
  0.0 1.9 %copy-start = (bf16[16,128,512]{2,1,0:T(8,128)(2,1)S(1)}, bf16[16,128,512]{2,1,0:T(8,128)(2,1)}, u32[]{:S(2)}) copy-start(bf16[16,128,512]{2,1,0:T(8,128)(2,1)} %param.17) | copy-start | bytes 6291460
  0.0 16.3 %collective-permute-start = (bf16[2048,8,56]{0,2,1:T(8,128)(2,1)}, bf16[2048,8,56]{0,2,1:T(8,128)(2,1)}, u32[]{:S(2)}, u32[]{:S(2)}) collective-permute-start(bf16[2048,8,56]{0,2,1:T(8,128)(2,1)} %param.19), channel_id=1, source_target_pairs={{0,8},{8,0},{1,9},{9,1},{2,10},{10,2},{3,11},{11,3},{4,12},{12,4},... | collective-permute-start | bytes 5505032 | tf_op jit(solution)/shard_map/ppermute | solution.py:36
  0.0 40.2 %collective-permute-start.2 = (bf16[896,1152]{1,0:T(8,128)(2,1)}, bf16[896,1152]{1,0:T(8,128)(2,1)}, u32[]{:S(2)}, u32[]{:S(2)}) collective-permute-start(bf16[896,1152]{1,0:T(8,128)(2,1)} %refs_4_.1), channel_id=1, source_target_pairs={{0,8},{8,0},{1,9},{9,1},{2,10},{10,2},{3,11},{11,3},{4,12},{12,4},... | collective-permute-start | bytes 6193160 | tf_op jit(solution)/shard_map/ppermute | solution.py:36
  0.5 39.7 %collective-permute-start.3 = (bf16[896,1152]{1,0:T(8,128)(2,1)}, bf16[896,1152]{1,0:T(8,128)(2,1)}, u32[]{:S(2)}, u32[]{:S(2)}) collective-permute-start(bf16[896,1152]{1,0:T(8,128)(2,1)} %refs_6_.1), channel_id=1, source_target_pairs={{0,8},{8,0},{1,9},{9,1},{2,10},{10,2},{3,11},{11,3},{4,12},{12,4},... | collective-permute-start | bytes 6193160 | tf_op jit(solution)/shard_map/ppermute | solution.py:36
  0.5 39.7 %collective-permute-start.4 = (bf16[1152,896]{1,0:T(8,128)(2,1)}, bf16[1152,896]{1,0:T(8,128)(2,1)}, u32[]{:S(2)}, u32[]{:S(2)}) collective-permute-start(bf16[1152,896]{1,0:T(8,128)(2,1)} %param.23), channel_id=1, source_target_pairs={{0,8},{8,0},{1,9},{9,1},{2,10},{10,2},{3,11},{11,3},{4,12},{12,4},... | collective-permute-start | bytes 6193160 | tf_op jit(solution)/shard_map/ppermute | solution.py:36
  3.5 20.3 %copy-start.5 = (bf16[32,896]{1,0:T(8,128)(2,1)S(1)}, bf16[32,896]{1,0:T(8,128)(2,1)}, u32[]{:S(2)}) copy-start(bf16[32,896]{1,0:T(8,128)(2,1)} %param.12) | copy-start | bytes 172036
  16.3 23.9 %all-to-all-start = ((bf16[8,32,2048]{2,1,0:T(8,128)(2,1)}), bf16[8,32,2048]{2,1,0:T(8,128)(2,1)S(1)}, u32[]{:S(2)}, u32[]{:S(2)}) async-start(bf16[8,32,2048]{2,1,0:T(8,128)(2,1)} %attend.1), calls=%async_computation | async-start | bytes 2097152 | tf_op jit(solution)/shard_map/all_to_all | solution.py:28
  23.7 16.5 %collective-permute-start.1 = (bf16[32,896]{1,0:T(8,128)(2,1)S(1)}, bf16[32,896]{1,0:T(8,128)(2,1)S(1)}, u32[]{:S(2)}, u32[]{:S(2)}) collective-permute-start(bf16[32,896]{1,0:T(8,128)(2,1)S(1)} %copy-done.5), channel_id=1, source_target_pairs={{0,16},{16,0},{1,17},{17,1},{2,18},{18,2},{3,19},{19,3},{4,20},{20... | collective-permute-start | bytes 172040 | tf_op jit(solution)/shard_map/ppermute | solution.py:303
  40.3 9.7 %copy-start.4 = (bf16[2,32,896]{2,1,0:T(8,128)(2,1)}, bf16[2,32,896]{2,1,0:T(8,128)(2,1)S(1)}, u32[]{:S(2)}) copy-start(bf16[2,32,896]{2,1,0:T(8,128)(2,1)S(1)} %pad_maximum_fusion.2.refs_0_) | copy-start | bytes 344068
  40.3 19.6 %collective-permute-start.7 = (bf16[2,32,896]{2,1,0:T(8,128)(2,1)S(1)}, bf16[2,32,896]{2,1,0:T(8,128)(2,1)S(1)}, u32[]{:S(2)}, u32[]{:S(2)}) collective-permute-start(bf16[2,32,896]{2,1,0:T(8,128)(2,1)S(1)} %pad_maximum_fusion.2.refs_0_), channel_id=1, source_target_pairs={{96,0},{0,32},{32,64},{64,96},{97,1},{1,33},{33,65},{65,97},{98,2}... | collective-permute-start | bytes 344072 | tf_op jit(solution)/shard_map/ppermute | solution.py:319
  41.8 18.0 %collective-permute-start.6 = (bf16[2,32,896]{2,1,0:T(8,128)(2,1)S(1)}, bf16[2,32,896]{2,1,0:T(8,128)(2,1)S(1)}, u32[]{:S(2)}, u32[]{:S(2)}) collective-permute-start(bf16[2,32,896]{2,1,0:T(8,128)(2,1)S(1)} %pad_maximum_fusion.2.refs_0_), channel_id=1, source_target_pairs={{64,0},{96,32},{0,64},{32,96},{65,1},{97,33},{1,65},{33,97},{66,2}... | collective-permute-start | bytes 344072 | tf_op jit(solution)/shard_map/ppermute | solution.py:319
  44.5 15.4 %collective-permute-start.5 = (bf16[2,32,896]{2,1,0:T(8,128)(2,1)S(1)}, bf16[2,32,896]{2,1,0:T(8,128)(2,1)}, u32[]{:S(2)}, u32[]{:S(2)}) collective-permute-start(bf16[2,32,896]{2,1,0:T(8,128)(2,1)S(1)} %pad_maximum_fusion.2.refs_0_), channel_id=1, source_target_pairs={{32,0},{64,32},{96,64},{0,96},{33,1},{65,33},{97,65},{1,97},{34,2}... | collective-permute-start | bytes 344072 | tf_op jit(solution)/shard_map/ppermute | solution.py:319
  49.9 14.1 %all-to-all-start.1 = ((bf16[8,2,56,256]{3,2,1,0:T(8,128)(2,1)}), bf16[8,2,56,256]{3,2,1,0:T(8,128)(2,1)S(1)}, u32[]{:S(2)}, u32[]{:S(2)}) async-start(bf16[8,2,56,256]{3,2,1,0:T(8,128)(2,1)} %fusion.2), calls=%async_computation.1 | async-start | bytes 917504 | tf_op jit(solution)/shard_map/all_to_all | solution.py:28
  55.3 13.3 %copy-start.8 = (bf16[896]{0:T(1024)(128)(2,1)S(1)}, bf16[896]{0:T(1024)(128)(2,1)}, u32[]{:S(2)}) copy-start(bf16[896]{0:T(1024)(128)(2,1)} %param.20) | copy-start | bytes 5380
  59.8 17.8 %copy-start.6 = (bf16[2,32,896]{2,1,0:T(8,128)(2,1)}, bf16[2,32,896]{2,1,0:T(8,128)(2,1)S(1)}, u32[]{:S(2)}) copy-start(bf16[2,32,896]{2,1,0:T(8,128)(2,1)S(1)} %collective-permute-done.7.refs_3_) | copy-start | bytes 344068
  59.8 17.8 %copy-start.7 = (bf16[2,32,896]{2,1,0:T(8,128)(2,1)}, bf16[2,32,896]{2,1,0:T(8,128)(2,1)S(1)}, u32[]{:S(2)}) copy-start(bf16[2,32,896]{2,1,0:T(8,128)(2,1)S(1)} %collective-permute-done.6.refs_2_) | copy-start | bytes 344068
  65.0 12.6 %all-to-all-start.2 = ((bf16[8,2,56,256]{3,2,1,0:T(8,128)(2,1)}), bf16[8,2,56,256]{3,2,1,0:T(8,128)(2,1)S(1)}, u32[]{:S(2)}, u32[]{:S(2)}) async-start(bf16[8,2,56,256]{3,2,1,0:T(8,128)(2,1)} %broadcast_in_dim.8), calls=%async_computation.2 | async-start | bytes 917504 | tf_op jit(solution)/shard_map/all_to_all | solution.py:24
  77.6 0.8 copy-start.2
  117.7 16.9 %copy-start.1 = (bf16[2304,896]{1,0:T(8,128)(2,1)S(1)}, bf16[2304,896]{1,0:T(8,128)(2,1)}, u32[]{:S(2)}) copy-start(bf16[2304,896]{1,0:T(8,128)(2,1)} %pad_maximum_fusion) | copy-start | bytes 12386308
  134.6 15.1 %copy-start.3 = (bf16[8,2,56,256]{3,2,1,0:T(8,128)(2,1)S(1)}, bf16[8,2,56,256]{3,2,1,0:T(8,128)(2,1)}, u32[]{:S(2)}) copy-start(bf16[8,2,56,256]{3,2,1,0:T(8,128)(2,1)} %copy-done.2) | copy-start | bytes 1376260
  136.8 12.9 %all-to-all-start.5 = ((bf16[8,32,896]{2,1,0:T(8,128)(2,1)}), bf16[8,32,896]{2,1,0:T(8,128)(2,1)S(1)}, u32[]{:S(2)}, u32[]{:S(2)}) async-start(bf16[8,32,896]{2,1,0:T(8,128)(2,1)} %bitcast.14), calls=%async_computation.5 | async-start | bytes 917504 | tf_op jit(solution)/shard_map/all_to_all | solution.py:28

commit v5 on v4

--- a/solution.py
+++ b/solution.py
@@ -47,7 +47,7 @@
 
     def kernel(places, attention_out, gain, *refs):
         pieces, sources = refs[:steps], refs[steps : steps + len(weights)]
-        out, ready, across_slot, slots, sums, power_slot, sems = refs[steps + len(weights) :]
+        out, own, ready, across_slot, whole, slots, sums, power_slot, sems = refs[steps + len(weights) :]
 
         def copy(i, source, target):
             return pltpu.make_async_copy(source, target, sems.at[i])
@@ -74,6 +74,8 @@
                 at = (x * sides + h) * rows
                 blocks.append(there.astype(F32) + across[at : at + rows])
         hidden = jnp.concatenate(blocks, axis=0)
+        whole[...] = hidden
+        own[...] = whole[pl.ds(pl.multiple_of((places[0] * sides + places[1]) * rows, rows), rows)]
         power = jnp.sum(hidden * hidden, axis=1, keepdims=True)
         high = power.astype(BF16).astype(F32)
         middle = (power - high).astype(BF16).astype(F32)
@@ -100,11 +102,15 @@
         kernel,
         in_specs=[pl.BlockSpec(memory_space=pltpu.SMEM), HBM, VMEM]
         + [HBM] * (steps + len(weights)),
-        out_specs=HBM,
-        out_shape=jax.ShapeDtypeStruct((tokens, len(weights) * units + LANES), BF16),
+        out_specs=(HBM, VMEM),
+        out_shape=(
+            jax.ShapeDtypeStruct((tokens, len(weights) * units + LANES), BF16),
+            jax.ShapeDtypeStruct((rows, width), F32),
+        ),
         scratch_shapes=[
             pltpu.VMEM((steps, sides, rows, width), BF16),
             pltpu.VMEM((width, tokens), BF16),
+            pltpu.VMEM((tokens, width), F32),
             pltpu.VMEM((len(weights), width, units), BF16),
             pltpu.VMEM((len(weights), tokens, units), BF16),
             pltpu.VMEM((tokens, LANES), BF16),
@@ -279,7 +285,6 @@
     rows = queries.shape[0]
     width = residual.shape[1]
     core = lax.axis_index("c")
-    chip = lax.axis_index(CHIPS)
     w_out_other = other_core(w_out)
     w_gate_other = other_core(w_gate)
     w_up_other = other_core(w_up)
@@ -297,16 +302,20 @@
         w_value,
         lax.axis_size(CHIPS),
     )
-    head_values, w_out_other = lax.optimization_barrier((head_values, w_out_other))
+    head_values, w_out_other, w_down_other = lax.optimization_barrier(
+        (head_values, w_out_other, w_down_other)
+    )
     w_out_both = jnp.stack([w_out, w_out_other], axis=2)
     all_values = exchange(head_values, CHIPS).reshape(-1, head_values.shape[2])
     across = lax.ppermute(residual, "h", [(0, 1), (1, 0)])
-    all_values, across, w_out_both, w_gate_other, w_up_other, w_down_other = (
+    w_down_both = jnp.concatenate([w_down, w_down_other], axis=0)
+    gain = norm_gain.astype(F32)[None, :]
+    places = jnp.stack([lax.axis_index("x"), lax.axis_index("h")])
+    all_values, w_out_both, w_down_both, w_gate_other, w_up_other, gain, places = (
         lax.optimization_barrier(
-            (all_values, across, w_out_both, w_gate_other, w_up_other, w_down_other)
+            (all_values, w_out_both, w_down_both, w_gate_other, w_up_other, gain, places)
         )
     )
-    w_down_both = jnp.concatenate([w_down, w_down_other], axis=0)
     tokens = all_values.shape[0]
 
     partial = jnp.einsum(
@@ -319,18 +328,16 @@
         lax.ppermute(both_rows, "x", [((i + step) % steps, i) for i in range(steps)])
         for step in range(1, steps)
     ]
-    arrived, w_down_both, *residuals = lax.optimization_barrier(
-        (arrived, w_down_both, *residuals)
-    )
+    arrived, *residuals = lax.optimization_barrier((arrived, *residuals))
     summed = arrived.astype(F32).sum(axis=0).astype(BF16)
     summed = jnp.where(core == 0, summed, summed[::-1])
     attention_cols = from_everyone(summed, CHIPS).reshape(width, tokens)
 
-    both = expand(
-        jnp.stack([lax.axis_index("x"), lax.axis_index("h")]),
+    both, own_hidden = expand(
+        places,
         residuals,
         attention_cols,
-        norm_gain.astype(F32)[None, :],
+        gain,
         (w_gate, w_gate_other, w_up, w_up_other),
     )
     both = exchange(both.reshape(lax.axis_size(HP), -1, both.shape[1]), HP)
@@ -346,12 +353,6 @@
     ffn = dot(activated, w_down_both, ((1,), (0,))).astype(BF16)
     ffn = exchange(ffn.reshape(-1, rows, width), CHIPS).astype(F32).sum(axis=0)
 
-    pick = (
-        lax.broadcasted_iota(jnp.int32, (tokens, rows), 0)
-        == lax.broadcasted_iota(jnp.int32, (tokens, rows), 1) + chip * rows
-    ).astype(BF16)
-    own_attention = dot(pick, attention_cols, ((0,), (1,)))
-    own_hidden = residual.astype(F32) + own_attention
     return (own_hidden + ffn).astype(BF16)
 
 

time: 151 us -> 151 us (level)
  blocking collectives: 48.2 us -> 73.4 us
  waiting for transfers between devices: 30 us -> 18.3 us
  starting transfers between devices: 30.4 us -> 19.7 us
  matrix products: 7.43 us -> 5.78 us
  local copies, waits for them, and re-layouts: 4.29 us -> 2.73 us
    all_to_all x1 -> x2, blocking collectives: 31.7 us -> 45.5 us  [exchange(): return lax.all_to_all(x, axes, 0, 0, tiled=True)]
    all_to_all x1 -> x2, blocking collectives: 16.5 us -> 27.9 us  [from_everyone(): lax.all_to_all(jnp.broadcast_to(x[None], (devices, *x.shape)), axes, 0, 0...]
    all_to_all x1 -> x0, waiting for transfers between devices: 7.78 us -> none  [from_everyone(): lax.all_to_all(jnp.broadcast_to(x[None], (devices, *x.shape)), axes, 0, 0...]
    all_to_all x3 -> x2, waiting for transfers between devices: 13.5 us -> 6.86 us  [exchange(): return lax.all_to_all(x, axes, 0, 0, tiled=True)]
    ppermute x3, waiting for transfers between devices: 0.01 us -> 5.68 us  [layer(): lax.ppermute(both_rows, 'x', [((i + step) % steps, i) for i in range(step...]
    all_to_all x3 -> x2, starting transfers between devices: 16.5 us -> 12.8 us  [exchange(): return lax.all_to_all(x, axes, 0, 0, tiled=True)]
    all_to_all x1 -> x0, starting transfers between devices: 3.65 us -> none  [from_everyone(): lax.all_to_all(jnp.broadcast_to(x[None], (devices, *x.shape)), axes, 0, 0...]
    ppermute x1, waiting for transfers between devices: 8.76 us -> 5.78 us  [layer(): across = lax.ppermute(residual, 'h', [(0, 1), (1, 0)])]
  transfers between devices with their start and end apart: 12 -> 10, of which waited for: 4 -> 5; matrix products, arithmetic and copies ran while one was open for 11% -> 8% of each run, Pallas kernels for 9% -> 8%
where the time goes in v5:
time: 151 us
  blocking collectives  73.4 us (49%)
  Pallas kernels  20.6 us (14%)
  starting transfers between devices  19.7 us (13%)
  waiting for transfers between devices  18.3 us (12%)
  other arithmetic  10.2 us (7%)
  matrix products  5.78 us (4%)
  local copies, waits for them, and re-layouts  2.73 us (2%)
    all_to_all x2, blocking collectives, exchange(): return lax.all_to_all(x, axes, 0, 0, tiled=True)  45.5 us
    all_to_all x2, blocking collectives, from_everyone(): lax.all_to_all(jnp.broadcast_to(x[None], (devices, *x.shape)), axes, 0, 0...  27.9 us
    all_to_all x2, starting transfers between devices, exchange(): return lax.all_to_all(x, axes, 0, 0, tiled=True)  12.8 us
    pallas_call x1, Pallas kernels, attend(): pl.pallas_call(kernel, in_specs=[pl.BlockSpec(memory_space=pltpu.SMEM), V...  12.8 us
    pallas_call x1, Pallas kernels, expand(): pl.pallas_call(kernel, in_specs=[pl.BlockSpec(memory_space=pltpu.SMEM), H...  7.85 us
    all_to_all x2, waiting for transfers between devices, exchange(): return lax.all_to_all(x, axes, 0, 0, tiled=True)  6.86 us
    ppermute x1, waiting for transfers between devices, layer(): across = lax.ppermute(residual, 'h', [(0, 1), (1, 0)])  5.78 us
    ppermute x3, waiting for transfers between devices, layer(): lax.ppermute(both_rows, 'x', [((i + step) % steps, i) for i in range(step...  5.68 us
  transfers between devices with their start and end apart: 10, of which 5 were waited for; matrix products, arithmetic and copies ran while one was open for 8% of the time, Pallas kernels for 8%

profile of v5, /device:TPU:0, one launch (start us, length us, event | category | flops | bytes accessed | tf_op | source)
XLA Modules:
  0.0 150.9 jit_solution(3380460806645804154)
XLA Ops:
  0.0 0.0 copy-start
  0.0 0.0 collective-permute-start.1
  0.0 0.5 collective-permute-start
  0.5 0.0 collective-permute-start.2
  0.5 0.5 collective-permute-start.3
  1.0 0.9 slice.12
  1.9 0.0 copy-done
  2.0 0.4 fusion.9
  2.4 1.1 copy.30
  3.4 0.0 copy-start.9
  3.5 12.8 %attend.1 = bf16[8,32,2048]{2,1,0:T(8,128)(2,1)} custom-call(s32[32]{0:T(128)} %lengths.1, bf16[32,16,512]{2,1,0:T(8,128)(2,1)} %bitcast.25, bf16[32,16,192]{2,1,0:T(8,128)(2,1)} %query.1, bf16[32,576]{1,0:T(8,128)(2,1)} %new.1, bf16[32,576,512]{2,1,0:T(8,128)(2,1)} %bitcast.23, bf16[16,512,128]{2,1,0:T(8,128)(2,1)} %w.1), custom_call_target="tpu_custom_call" | custom-call | flops 603979776 | bytes 18874368 | tf_op jit(solution)/shard_map/attend/pallas_call | solution.py:247
  16.2 0.0 collective-permute-done
  16.2 0.0 collective-permute-done.1
  16.3 7.4 %all-to-all-start = ((bf16[8,32,2048]{2,1,0:T(8,128)(2,1)}), bf16[8,32,2048]{2,1,0:T(8,128)(2,1)S(1)}, u32[]{:S(2)}, u32[]{:S(2)}) async-start(bf16[8,32,2048]{2,1,0:T(8,128)(2,1)} %attend.1), calls=%async_computation | async-start | bytes 2097152 | tf_op jit(solution)/shard_map/all_to_all | solution.py:28
  23.7 0.0 copy-done.9
  23.7 0.6 reshape.30.gain
  24.3 0.6 pad_add_fusion.places
  24.9 0.0 copy-start.2
  24.9 4.3 %pad_maximum_fusion.1 = bf16[2048,8,2,56]{0,3,1,2:T(8,128)(2,1)} fusion(bf16[2048,8,1,56]{0,3,1,2:T(8,128)(2,1)} %bitcast.4, bf16[2048,8,1,56]{0,3,1,2:T(8,128)(2,1)} %bitcast.26), kind=kLoop, calls=%fused_computation.2 | loop fusion | flops 1835008 | bytes 7340032 | tf_op jit(solution)/shard_map/stack | solution.py:308
  29.2 0.0 copy-done.2
  29.2 3.8 %pad_maximum_fusion = bf16[2304,896]{1,0:T(8,128)(2,1)} fusion(bf16[1152,896]{1,0:T(8,128)(2,1)} %collective-permute-done.1, bf16[1152,896]{1,0:T(8,128)(2,1)S(1)} %copy-done.2), kind=kLoop, calls=%fused_computation.1 | loop fusion | flops 8257536 | bytes 8257536 | tf_op jit(solution)/shard_map/concatenate | solution.py:311
  33.0 0.0 collective-permute-done.2.refs_5_
  33.0 0.0 collective-permute-done.3.refs_7_
  33.1 6.9 %all-to-all-done = bf16[8,32,2048]{2,1,0:T(8,128)(2,1)S(1)} async-done(((bf16[8,32,2048]{2,1,0:T(8,128)(2,1)}), bf16[8,32,2048]{2,1,0:T(8,128)(2,1)S(1)}, u32[]{:S(2)}, u32[]{:S(2)}) %all-to-all-start) | async-done | bytes 1048608 | tf_op jit(solution)/shard_map/all_to_all | solution.py:28
  39.9 0.0 copy-start.8
  39.9 4.0 %fusion.2 = bf16[8,2,56,256]{3,2,1,0:T(8,128)(2,1)} fusion(bf16[2048,8,2,56]{0,3,1,2:T(8,128)(2,1)} %pad_maximum_fusion.1, bf16[256,2048]{1,0:T(8,128)(2,1)S(1)} %bitcast.29), kind=kOutput, calls=%fused_computation.6 | convolution fusion | flops 939753472 | bytes 5177344 | tf_op jit(solution)/shard_map/tk,kbcf->bcft/dot_general | solution.py:321
  43.9 5.4 %all-to-all-start.1 = ((bf16[8,2,56,256]{3,2,1,0:T(8,128)(2,1)}), bf16[8,2,56,256]{3,2,1,0:T(8,128)(2,1)S(1)}, u32[]{:S(2)}, u32[]{:S(2)}) async-start(bf16[8,2,56,256]{3,2,1,0:T(8,128)(2,1)} %fusion.2), calls=%async_computation.1 | async-start | bytes 917504 | tf_op jit(solution)/shard_map/all_to_all | solution.py:28
  49.3 0.0 copy-done.8
  49.3 2.7 %collective-permute-start.4 = (bf16[32,896]{1,0:T(8,128)(2,1)S(1)}, bf16[32,896]{1,0:T(8,128)(2,1)S(1)}, u32[]{:S(2)}, u32[]{:S(2)}) collective-permute-start(bf16[32,896]{1,0:T(8,128)(2,1)S(1)} %copy-done.8), channel_id=1, source_target_pairs={{0,16},{16,0},{1,17},{17,1},{2,18},{18,2},{3,19},{19,3},{4,20},{20... | collective-permute-start | bytes 172040 | tf_op jit(solution)/shard_map/ppermute | solution.py:310
  52.1 5.8 %collective-permute-done.4 = bf16[32,896]{1,0:T(8,128)(2,1)S(1)} collective-permute-done((bf16[32,896]{1,0:T(8,128)(2,1)S(1)}, bf16[32,896]{1,0:T(8,128)(2,1)S(1)}, u32[]{:S(2)}, u32[]{:S(2)}) %collective-permute-start.4) | collective-permute-done | bytes 57376 | tf_op jit(solution)/shard_map/ppermute | solution.py:310
  57.9 0.0 copy-start.3
  57.9 1.2 collective-permute-start.5
  59.1 1.5 collective-permute-start.6
  60.6 0.3 collective-permute-start.7
  60.9 1.8 %collective-permute-done.5.refs_1_ = bf16[2,32,896]{2,1,0:T(8,128)(2,1)S(1)} collective-permute-done((bf16[2,32,896]{2,1,0:T(8,128)(2,1)S(1)}, bf16[2,32,896]{2,1,0:T(8,128)(2,1)S(1)}, u32[]{:S(2)}, u32[]{:S(2)}) %collective-permute-start.5) | collective-permute-done | bytes 114720 | tf_op jit(solution)/shard_map/ppermute | solution.py:328
  62.7 0.0 copy-start.4
  62.7 2.6 %collective-permute-done.6.refs_2_ = bf16[2,32,896]{2,1,0:T(8,128)(2,1)S(1)} collective-permute-done((bf16[2,32,896]{2,1,0:T(8,128)(2,1)S(1)}, bf16[2,32,896]{2,1,0:T(8,128)(2,1)S(1)}, u32[]{:S(2)}, u32[]{:S(2)}) %collective-permute-start.6) | collective-permute-done | bytes 114720 | tf_op jit(solution)/shard_map/ppermute | solution.py:328
  65.4 0.0 copy-start.5
  65.4 1.2 collective-permute-done.7.refs_3_
  66.6 0.0 copy-start.6
  66.6 0.0 all-to-all-done.1
  66.6 0.1 reduce_sum.39
  66.8 12.9 %all_to_all.30 = bf16[8,2,56,256]{3,2,1,0:T(8,128)(2,1)} all-to-all(bf16[8,2,56,256]{3,2,1,0:T(8,128)(2,1)S(1)} %broadcast_in_dim.21), channel_id=1, replica_groups=mesh['x'=4,'h'=2,'c'=2,'z'=4,'l'=2] {'x','h'}, dimensions={0} | all-to-all | bytes 917504 | tf_op jit(solution)/shard_map/all_to_all | solution.py:24
  79.7 0.0 copy-done.3
  79.7 0.0 copy-done.4
  79.7 0.0 copy-done.5
  79.7 0.0 copy-done.6
  79.7 7.9 %expand.1 = (bf16[256,4736]{1,0:T(8,128)(2,1)}, f32[32,896]{1,0:T(8,128)}) custom-call(s32[2]{0:T(128)} %pad_add_fusion.places, bf16[896,256]{1,0:T(8,128)(2,1)} %bitcast.27, f32[1,896]{1,0:T(1,128)} %reshape.30.gain, bf16[2,32,896]{2,1,0:T(8,128)(2,1)} %copy-done.3, bf16[2,32,896]{2,1,0:T(8,128)(2,1)} %copy-done.4, bf16[2,32,896]{2,1,0:T(8,128)(2,1)} %copy-done.5, ...), custom_call_target="tpu_custom_call" | custom-call | tf_op jit(solution)/shard_map/expand/pallas_call | solution.py:101
  87.5 31.9 %all_to_all.31 = bf16[8,32,4736]{2,1,0:T(8,128)(2,1)S(1)} all-to-all(bf16[8,32,4736]{2,1,0:T(8,128)(2,1)} %bitcast.24), channel_id=1, replica_groups=mesh['x'=4,'h'=2,'c'=2,'z'=4,'l'=2] {'z','l'}, dimensions={0} | all-to-all | bytes 4849664 | tf_op jit(solution)/shard_map/all_to_all | solution.py:28
  119.5 0.3 convert_reduce_fusion
  119.8 0.0 copy-start.1
  119.8 0.1 slice_reduce_fusion
  119.9 0.2 fusion.8
  120.1 0.1 broadcast_in_dim.22
  120.2 15.0 %all_to_all.32 = bf16[8,32,2304]{2,1,0:T(8,128)(2,1)S(1)} all-to-all(bf16[8,32,2304]{2,1,0:T(8,128)(2,1)S(1)} %broadcast_in_dim.22), channel_id=1, replica_groups=mesh['x'=4,'h'=2,'c'=2,'z'=4,'l'=2] {'z','l'}, dimensions={0} | all-to-all | bytes 2359296 | tf_op jit(solution)/shard_map/all_to_all | solution.py:24
  135.2 0.0 copy-done.1
  135.2 0.0 copy-start.7
  135.2 1.4 convolution_convert_fusion
  136.6 13.6 %all_to_all.33 = bf16[8,32,896]{2,1,0:T(8,128)(2,1)S(1)} all-to-all(bf16[8,32,896]{2,1,0:T(8,128)(2,1)S(1)} %bitcast.30), channel_id=1, replica_groups=mesh['x'=4,'h'=2,'c'=2,'z'=4,'l'=2] {'x','h'}, dimensions={0} | all-to-all | bytes 917504 | tf_op jit(solution)/shard_map/all_to_all | solution.py:28
  150.2 0.1 convert_reduce_fusion.1
  150.3 0.0 copy-done.7
  150.3 0.6 add_convert_fusion
  (4 shorter events, 0.1 us)
Async XLA Ops:
  0.0 1.9 %copy-start = (bf16[16,128,512]{2,1,0:T(8,128)(2,1)S(1)}, bf16[16,128,512]{2,1,0:T(8,128)(2,1)}, u32[]{:S(2)}) copy-start(bf16[16,128,512]{2,1,0:T(8,128)(2,1)} %param.17) | copy-start | bytes 6291460
  0.0 16.2 %collective-permute-start.1 = (bf16[1152,896]{1,0:T(8,128)(2,1)}, bf16[1152,896]{1,0:T(8,128)(2,1)}, u32[]{:S(2)}, u32[]{:S(2)}) collective-permute-start(bf16[1152,896]{1,0:T(8,128)(2,1)} %param.23), channel_id=1, source_target_pairs={{0,8},{8,0},{1,9},{9,1},{2,10},{10,2},{3,11},{11,3},{4,12},{12,4},... | collective-permute-start | bytes 6193160 | tf_op jit(solution)/shard_map/ppermute | solution.py:36
  0.0 16.2 %collective-permute-start = (bf16[2048,8,56]{0,2,1:T(8,128)(2,1)}, bf16[2048,8,56]{0,2,1:T(8,128)(2,1)}, u32[]{:S(2)}, u32[]{:S(2)}) collective-permute-start(bf16[2048,8,56]{0,2,1:T(8,128)(2,1)} %param.19), channel_id=1, source_target_pairs={{0,8},{8,0},{1,9},{9,1},{2,10},{10,2},{3,11},{11,3},{4,12},{12,4},... | collective-permute-start | bytes 5505032 | tf_op jit(solution)/shard_map/ppermute | solution.py:36
  0.5 32.5 %collective-permute-start.2 = (bf16[896,1152]{1,0:T(8,128)(2,1)}, bf16[896,1152]{1,0:T(8,128)(2,1)}, u32[]{:S(2)}, u32[]{:S(2)}) collective-permute-start(bf16[896,1152]{1,0:T(8,128)(2,1)} %refs_4_.1), channel_id=1, source_target_pairs={{0,8},{8,0},{1,9},{9,1},{2,10},{10,2},{3,11},{11,3},{4,12},{12,4},... | collective-permute-start | bytes 6193160 | tf_op jit(solution)/shard_map/ppermute | solution.py:36
  0.5 32.5 %collective-permute-start.3 = (bf16[896,1152]{1,0:T(8,128)(2,1)}, bf16[896,1152]{1,0:T(8,128)(2,1)}, u32[]{:S(2)}, u32[]{:S(2)}) collective-permute-start(bf16[896,1152]{1,0:T(8,128)(2,1)} %refs_6_.1), channel_id=1, source_target_pairs={{0,8},{8,0},{1,9},{9,1},{2,10},{10,2},{3,11},{11,3},{4,12},{12,4},... | collective-permute-start | bytes 6193160 | tf_op jit(solution)/shard_map/ppermute | solution.py:36
  3.4 20.2 %copy-start.9 = (bf16[896]{0:T(1024)(128)(2,1)S(1)}, bf16[896]{0:T(1024)(128)(2,1)}, u32[]{:S(2)}) copy-start(bf16[896]{0:T(1024)(128)(2,1)} %param.20) | copy-start | bytes 5380
  16.3 23.6 %all-to-all-start = ((bf16[8,32,2048]{2,1,0:T(8,128)(2,1)}), bf16[8,32,2048]{2,1,0:T(8,128)(2,1)S(1)}, u32[]{:S(2)}, u32[]{:S(2)}) async-start(bf16[8,32,2048]{2,1,0:T(8,128)(2,1)} %attend.1), calls=%async_computation | async-start | bytes 2097152 | tf_op jit(solution)/shard_map/all_to_all | solution.py:28
  24.9 4.3 %copy-start.2 = (bf16[1152,896]{1,0:T(8,128)(2,1)S(1)}, bf16[1152,896]{1,0:T(8,128)(2,1)}, u32[]{:S(2)}) copy-start(bf16[1152,896]{1,0:T(8,128)(2,1)} %param.23) | copy-start | bytes 6193156
  39.9 9.4 %copy-start.8 = (bf16[32,896]{1,0:T(8,128)(2,1)S(1)}, bf16[32,896]{1,0:T(8,128)(2,1)}, u32[]{:S(2)}) copy-start(bf16[32,896]{1,0:T(8,128)(2,1)} %param.12) | copy-start | bytes 172036
  43.9 22.7 %all-to-all-start.1 = ((bf16[8,2,56,256]{3,2,1,0:T(8,128)(2,1)}), bf16[8,2,56,256]{3,2,1,0:T(8,128)(2,1)S(1)}, u32[]{:S(2)}, u32[]{:S(2)}) async-start(bf16[8,2,56,256]{3,2,1,0:T(8,128)(2,1)} %fusion.2), calls=%async_computation.1 | async-start | bytes 917504 | tf_op jit(solution)/shard_map/all_to_all | solution.py:28
  49.3 8.5 %collective-permute-start.4 = (bf16[32,896]{1,0:T(8,128)(2,1)S(1)}, bf16[32,896]{1,0:T(8,128)(2,1)S(1)}, u32[]{:S(2)}, u32[]{:S(2)}) collective-permute-start(bf16[32,896]{1,0:T(8,128)(2,1)S(1)} %copy-done.8), channel_id=1, source_target_pairs={{0,16},{16,0},{1,17},{17,1},{2,18},{18,2},{3,19},{19,3},{4,20},{20... | collective-permute-start | bytes 172040 | tf_op jit(solution)/shard_map/ppermute | solution.py:310
  57.9 21.8 %copy-start.3 = (bf16[2,32,896]{2,1,0:T(8,128)(2,1)}, bf16[2,32,896]{2,1,0:T(8,128)(2,1)S(1)}, u32[]{:S(2)}) copy-start(bf16[2,32,896]{2,1,0:T(8,128)(2,1)S(1)} %pad_maximum_fusion.2.refs_0_) | copy-start | bytes 344068
  57.9 4.9 %collective-permute-start.5 = (bf16[2,32,896]{2,1,0:T(8,128)(2,1)S(1)}, bf16[2,32,896]{2,1,0:T(8,128)(2,1)S(1)}, u32[]{:S(2)}, u32[]{:S(2)}) collective-permute-start(bf16[2,32,896]{2,1,0:T(8,128)(2,1)S(1)} %pad_maximum_fusion.2.refs_0_), channel_id=1, source_target_pairs={{32,0},{64,32},{96,64},{0,96},{33,1},{65,33},{97,65},{1,97},{34,2}... | collective-permute-start | bytes 344072 | tf_op jit(solution)/shard_map/ppermute | solution.py:328
  59.1 6.3 %collective-permute-start.6 = (bf16[2,32,896]{2,1,0:T(8,128)(2,1)S(1)}, bf16[2,32,896]{2,1,0:T(8,128)(2,1)S(1)}, u32[]{:S(2)}, u32[]{:S(2)}) collective-permute-start(bf16[2,32,896]{2,1,0:T(8,128)(2,1)S(1)} %pad_maximum_fusion.2.refs_0_), channel_id=1, source_target_pairs={{64,0},{96,32},{0,64},{32,96},{65,1},{97,33},{1,65},{33,97},{66,2}... | collective-permute-start | bytes 344072 | tf_op jit(solution)/shard_map/ppermute | solution.py:328
  60.6 6.0 %collective-permute-start.7 = (bf16[2,32,896]{2,1,0:T(8,128)(2,1)S(1)}, bf16[2,32,896]{2,1,0:T(8,128)(2,1)S(1)}, u32[]{:S(2)}, u32[]{:S(2)}) collective-permute-start(bf16[2,32,896]{2,1,0:T(8,128)(2,1)S(1)} %pad_maximum_fusion.2.refs_0_), channel_id=1, source_target_pairs={{96,0},{0,32},{32,64},{64,96},{97,1},{1,33},{33,65},{65,97},{98,2}... | collective-permute-start | bytes 344072 | tf_op jit(solution)/shard_map/ppermute | solution.py:328
  62.7 16.9 %copy-start.4 = (bf16[2,32,896]{2,1,0:T(8,128)(2,1)}, bf16[2,32,896]{2,1,0:T(8,128)(2,1)S(1)}, u32[]{:S(2)}) copy-start(bf16[2,32,896]{2,1,0:T(8,128)(2,1)S(1)} %collective-permute-done.5.refs_1_) | copy-start | bytes 344068
  65.4 14.3 %copy-start.5 = (bf16[2,32,896]{2,1,0:T(8,128)(2,1)}, bf16[2,32,896]{2,1,0:T(8,128)(2,1)S(1)}, u32[]{:S(2)}) copy-start(bf16[2,32,896]{2,1,0:T(8,128)(2,1)S(1)} %collective-permute-done.6.refs_2_) | copy-start | bytes 344068
  66.6 13.0 %copy-start.6 = (bf16[2,32,896]{2,1,0:T(8,128)(2,1)}, bf16[2,32,896]{2,1,0:T(8,128)(2,1)S(1)}, u32[]{:S(2)}) copy-start(bf16[2,32,896]{2,1,0:T(8,128)(2,1)S(1)} %collective-permute-done.7.refs_3_) | copy-start | bytes 344068
  119.8 15.4 %copy-start.1 = (bf16[2304,896]{1,0:T(8,128)(2,1)S(1)}, bf16[2304,896]{1,0:T(8,128)(2,1)}, u32[]{:S(2)}) copy-start(bf16[2304,896]{1,0:T(8,128)(2,1)} %pad_maximum_fusion) | copy-start | bytes 12386308
  135.2 15.0 %copy-start.7 = (f32[32,896]{1,0:T(8,128)S(1)}, f32[32,896]{1,0:T(8,128)}, u32[]{:S(2)}) copy-start(f32[32,896]{1,0:T(8,128)} %get-tuple-element.36) | copy-start | bytes 344068
